TPU v7x, 256 devices: a whole 4x4x8 slice. The times are simulated.
256 devices in a mesh: seq: 32 (over z_lo, y, core), head: 8 (over z_hi, x).
Axes of the slice: x: 4, y: 4, z: 8 (z_hi: 2, z_lo: 4; z = z_hi * 4 + z_lo), core: 2. Of those that a mesh axis runs over, the one named last changes fastest.
Arguments:
- fast_q: bfloat16 [8192, 4096], P('seq', 'head'), may hold values from -6 to 6
- fast_k: bfloat16 [8192, 4096], P('seq', 'head'), may hold values from -6 to 6
- fast_v: bfloat16 [8192, 4096], P('seq', 'head'), may hold values from -6 to 6
- rates: float32 [8, 8192], P('head', 'seq'), may hold values from 0.02 to 1
- w_gate: bfloat16 [8, 512, 512], P('head'), may hold values from -0.25 to 0.25
- w_up: bfloat16 [8, 512, 512], P('head'), may hold values from -0.25 to 0.25
- w_down: bfloat16 [8, 512, 512], P('head'), may hold values from -0.25 to 0.25
- w_out: bfloat16 [4096, 5120], P('head'), may hold values from -0.09375 to 0.09375
- att_q: bfloat16 [8192, 5120], P('seq', 'head'), may hold values from -5 to 5
- att_k: bfloat16 [8192, 5120], P('seq', 'head'), may hold values from -5 to 5
- att_v: bfloat16 [8192, 5120], P('seq', 'head'), may hold values from -6 to 6
Outputs:
- mixed: bfloat16 [8192, 5120], P('seq', 'head')
- final_weights: bfloat16 [3, 8, 512, 512], P(None, 'head', 'seq')
All inputs are finite; a program needn't handle non-finite values.
Results may differ from a plain program's by a relative error of at most 0.022.
Values may be sent and summed in bfloat16 or wider, within the bound.
No kernel may reach another device: no remote copies, remote signals or barrier semaphores. Data moves between devices by JAX's collectives and lax.ppermute only.
A program may use at most 64 MiB of HBM per device.

v0:
```python
import jax
import jax.numpy as jnp
from jax import lax
from jax.experimental import pallas as pl
from jax.experimental.pallas import tpu as pltpu
from jax.sharding import Mesh
from jax.sharding import PartitionSpec as P

AD = 128
NS_STEPS = 2
NEWTON_COEFFS = (3.4445, -4.775, 2.0315)
SEQ = ("span", "row", "y", "core")
CHIPS = ("row", "y")
HEAD = ("head_0", "head_1")
F32 = jnp.float32
BF16 = jnp.bfloat16


VMEM = pl.BlockSpec(memory_space=pltpu.VMEM)
SMEM = pl.BlockSpec(memory_space=pltpu.SMEM)
ANY = pl.BlockSpec(memory_space=pl.ANY)


def nn(a, b):
    return lax.dot_general(a, b, (((1,), (0,)), ((), ())), preferred_element_type=F32)


def nt(a, b):
    return lax.dot_general(a, b, (((1,), (1,)), ((), ())), preferred_element_type=F32)


def tn(a, b):
    return lax.dot_general(a, b, (((0,), (0,)), ((), ())), preferred_element_type=F32)


def call(kernel, outs, args, scratch=(), smem=0):
    return pl.pallas_call(
        kernel,
        out_shape=outs,
        in_specs=[SMEM] * smem + [VMEM] * (len(args) - smem),
        out_specs=jax.tree.map(lambda _: VMEM, outs),
        scratch_shapes=scratch,
    )(*args)


def start(source, target, sem):
    copy = pltpu.make_async_copy(source, target, sem)
    copy.start()
    return copy


def split_gradients(core, k, v, rate, weights, own_ref, far_ref, own_out, far_out, sem):
    weighted = (rate * v.astype(F32)).astype(BF16)
    x = nn(k, weights[0])
    u = nn(k, weights[1])
    sig = jax.nn.sigmoid(x)
    silu = x * sig
    neg_act = (-(silu * u)).astype(BF16)
    copies = []

    def emit(m, left, right):
        _, blocks, step, _ = own_ref.shape
        half = blocks * step
        for h in range(2):
            g = tn(left[:, h * half : (h + 1) * half], right).astype(BF16).reshape(own_ref.shape[1:])

            @pl.when(core == h)
            def _():
                own_ref[m] = g

            @pl.when(core != h)
            def _():
                far_ref[m] = g

        copies.append(start(own_ref.at[m], own_out.at[:, m], sem.at[m]))
        copies.append(start(far_ref.at[m], far_out.at[:, m], sem.at[3 + m]))

    emit(2, neg_act, weighted)
    back = -nt(weighted, weights[2])
    emit(1, k, (back * silu).astype(BF16))
    emit(0, k, (back * u * (sig * (1.0 + x * (1.0 - sig)))).astype(BF16))
    return copies


def column(row):
    size = row.shape[1]
    eye = lax.broadcasted_iota(jnp.int32, (size, size), 0) == lax.broadcasted_iota(
        jnp.int32, (size, size), 1
    )
    return jnp.sum(jnp.where(eye, row, 0.0), axis=1, keepdims=True)


def gradients_kernel(
    core_ref, rate_ref, k_in, v_in, wg_in, wu_in, wd_in, own_out, far_out,
    k_ref, v_ref, w_ref, own_ref, far_ref, sem, out_sem,
):
    loads = [
        start(source, target, sem.at[i])
        for i, (source, target) in enumerate(
            (
                (k_in, k_ref),
                (wg_in.at[0], w_ref.at[0]),
                (wu_in.at[0], w_ref.at[1]),
                (v_in, v_ref),
                (wd_in.at[0], w_ref.at[2]),
            )
        )
    ]
    rate = column(rate_ref[...])
    for copy in loads:
        copy.wait()
    weights = [w_ref[m] for m in range(3)]
    for copy in split_gradients(
        core_ref[0], k_ref[...], v_ref[...], rate, weights, own_ref, far_ref, own_out, far_out, out_sem
    ):
        copy.wait()


def split_shape(features, blocks):
    return (blocks, 3, features // 2 // blocks, features)


def split_scratch(features, blocks):
    return [pltpu.VMEM((3, blocks, features // 2 // blocks, features), BF16)] * 2


def gradients(core, k, v, rate, weights, blocks):
    rows, features = k.shape
    shape = jax.ShapeDtypeStruct(split_shape(features, blocks), BF16)
    return pl.pallas_call(
        gradients_kernel,
        out_shape=(shape, shape),
        in_specs=[SMEM, VMEM] + [ANY] * 5,
        out_specs=(ANY, ANY),
        scratch_shapes=[
            pltpu.VMEM((rows, features), BF16),
            pltpu.VMEM((rows, features), BF16),
            pltpu.VMEM((3, features, features), BF16),
            *split_scratch(features, blocks),
            pltpu.SemaphoreType.DMA((5,)),
            pltpu.SemaphoreType.DMA((6,)),
        ],
    )(core, rate, k, v, *weights)


def orthogonal(gradients):
    first, second, third = NEWTON_COEFFS
    xs = []
    for load in gradients:
        wide = load().astype(F32)
        xs.append((wide * lax.rsqrt(jnp.sum(wide * wide) + 1e-6)).astype(BF16))
    for _ in range(NS_STEPS):
        grams = [nt(x, x).astype(BF16) for x in xs]
        polys = [(second * g.astype(F32) + third * nn(g, g)).astype(BF16) for g in grams]
        xs = [(first * x.astype(F32) + nn(p, x)).astype(BF16) for p, x in zip(polys, xs)]
    return xs


def moved_weight(w, x):
    w = w.astype(F32)
    moved = w - x.astype(F32)
    target = jnp.sqrt(jnp.sum(w * w, axis=0, keepdims=True) + 1e-6)
    current = jnp.sqrt(jnp.sum(moved * moved, axis=0, keepdims=True) + 1e-6)
    return (moved * (target / current)).astype(BF16)


def gathered(core, own_in, far_in, g_ref, sem):
    loads = []

    def wanted(m, pair):
        def load():
            for copy in pair:
                copy.wait()
            return g_ref[m].reshape(g_ref.shape[4], g_ref.shape[4])

        return load

    for m in range(3):
        pair = (
            start(own_in.at[:, m], g_ref.at[m, core], sem.at[m]),
            start(far_in.at[:, m], g_ref.at[m, 1 - core], sem.at[3 + m]),
        )
        loads.append(wanted(m, pair))
    return loads


def update_kernel(
    core_ref, rate_ref, own_in, far_in, wg_in, wu_in, wd_in, k_in, v_in,
    wg_out, wu_out, wd_out, own_out, far_out,
    g_ref, w_ref, k_ref, v_ref, own_ref, far_ref, sem, g_sem, w_sem, out_sem,
):
    core = core_ref[0]
    loads = gathered(core, own_in, far_in, g_ref, g_sem)
    others = [start(w.at[0], w_ref.at[m], sem.at[m]) for m, w in enumerate((wg_in, wu_in, wd_in))]
    others += [start(k_in, k_ref, sem.at[3]), start(v_in, v_ref, sem.at[4])]
    rate = column(rate_ref[...])
    xs = orthogonal(loads)
    for copy in others:
        copy.wait()
    weights = [moved_weight(w_ref[m], x) for m, x in enumerate(xs)]
    copies = []
    for m, (w, out) in enumerate(zip(weights, (wg_out, wu_out, wd_out))):
        w_ref[m] = w
        copies.append(start(w_ref.at[m], out.at[0], w_sem.at[m]))
    copies += split_gradients(
        core, k_ref[...], v_ref[...], rate, weights, own_ref, far_ref, own_out, far_out, out_sem
    )
    for copy in copies:
        copy.wait()


def update(core, rate, own, far, weights, k, v):
    rows, features = k.shape
    blocks, _, step, _ = own.shape
    weight = jax.ShapeDtypeStruct(weights[0].shape, BF16)
    split = jax.ShapeDtypeStruct(own.shape, BF16)
    out = pl.pallas_call(
        update_kernel,
        out_shape=(weight,) * 3 + (split,) * 2,
        in_specs=[SMEM, VMEM] + [ANY] * 7,
        out_specs=(ANY,) * 5,
        scratch_shapes=[
            pltpu.VMEM((3, 2, blocks, step, features), BF16),
            pltpu.VMEM((3, features, features), BF16),
            pltpu.VMEM((rows, features), BF16),
            pltpu.VMEM((rows, features), BF16),
            *split_scratch(features, blocks),
            pltpu.SemaphoreType.DMA((5,)),
            pltpu.SemaphoreType.DMA((6,)),
            pltpu.SemaphoreType.DMA((3,)),
            pltpu.SemaphoreType.DMA((6,)),
        ],
    )(core, rate, own, far, *weights, k, v)
    return out[:3], out[3], out[4]


def last_kernel(
    core_ref, seat_ref, own_in, far_in, wg_in, wu_in, wd_in, mine_ref, peer_ref, g_ref, w_ref, sem, g_sem
):
    seat = seat_ref[0]
    loads = gathered(core_ref[0], own_in, far_in, g_ref, g_sem)
    others = [start(w.at[0], w_ref.at[m], sem.at[m]) for m, w in enumerate((wg_in, wu_in, wd_in))]
    share = mine_ref.shape[1]
    half = w_ref.shape[1] // 2
    xs = orthogonal(loads)
    for copy in others:
        copy.wait()
    for m, x in enumerate(xs):
        w_ref[m] = moved_weight(w_ref[m], x)
        peer_ref[m] = w_ref[m, pl.ds(pl.multiple_of(seat * share, share), share), :]
        mine_ref[m] = w_ref[m, pl.ds(pl.multiple_of(half + seat * share, share), share), :]


def last_update(core, seat, own, far, weights, share):
    blocks, _, step, features = own.shape
    shape = jax.ShapeDtypeStruct((3, share, features), BF16)
    return pl.pallas_call(
        last_kernel,
        out_shape=(shape, shape),
        in_specs=[SMEM, SMEM] + [ANY] * 5,
        out_specs=(VMEM, VMEM),
        scratch_shapes=[
            pltpu.VMEM((3, 2, blocks, step, features), BF16),
            pltpu.VMEM((3, features, features), BF16),
            pltpu.SemaphoreType.DMA((3,)),
            pltpu.SemaphoreType.DMA((6,)),
        ],
    )(core, seat, own, far, *weights)


def blocks_of(wo_in, blocks_ref, wo_ref, sem):
    columns = wo_ref.shape[2]
    return [
        start(
            wo_in.at[:, pl.ds(pl.multiple_of(blocks_ref[i] * columns, 128), columns)], wo_ref.at[i], sem.at[i]
        )
        for i in range(4)
    ]


def products(rows, loads, wo_ref, part_ref, a_out, b_out, sem):
    copies = []
    for i in range(4):
        loads[i].wait()
        part_ref[i] = nn(rows, wo_ref[i]).astype(BF16)
        copies.append(start(part_ref.at[i], (a_out, b_out)[i // 2].at[i % 2], sem.at[i]))
    for copy in copies:
        copy.wait()


def first_products_kernel(
    blocks_ref, q_in, wg_in, wu_in, wd_in, wo_in, a_out, b_out, rows_out,
    q_ref, w_ref, wo_ref, rows_ref, part_ref, sem, wo_sem, out_sem,
):
    inputs = [start(q_in, q_ref, sem.at[3])]
    inputs += [start(w.at[0], w_ref.at[m], sem.at[m]) for m, w in enumerate((wg_in, wu_in, wd_in))]
    loads = blocks_of(wo_in, blocks_ref, wo_ref, wo_sem)
    for copy in inputs:
        copy.wait()
    q = q_ref[...]
    x = nn(q, w_ref[0])
    act = (jax.nn.silu(x) * nn(q, w_ref[1])).astype(BF16)
    raw = nn(act, w_ref[2])
    rows = (raw * lax.rsqrt(jnp.mean(raw * raw, axis=-1, keepdims=True) + 1e-6)).astype(BF16)
    rows_ref[...] = rows
    kept = start(rows_ref, rows_out, sem.at[4])
    products(rows, loads, wo_ref, part_ref, a_out, b_out, out_sem)
    kept.wait()


def later_products_kernel(
    blocks_ref, rows_in, wo_in, a_out, b_out, wo_ref, rows_ref, part_ref, sem, wo_sem, out_sem
):
    kept = start(rows_in, rows_ref, sem)
    loads = blocks_of(wo_in, blocks_ref, wo_ref, wo_sem)
    kept.wait()
    products(rows_ref[...], loads, wo_ref, part_ref, a_out, b_out, out_sem)


def first_products(blocks, q, weights, w_out, heads):
    rows, features = q.shape
    columns = w_out.shape[1] // heads
    pair = jax.ShapeDtypeStruct((2, rows, columns), BF16)
    return pl.pallas_call(
        first_products_kernel,
        out_shape=(pair, pair, jax.ShapeDtypeStruct((rows, features), BF16)),
        in_specs=[SMEM] + [ANY] * 5,
        out_specs=(ANY,) * 3,
        scratch_shapes=[
            pltpu.VMEM((rows, features), BF16),
            pltpu.VMEM((3, features, features), BF16),
            pltpu.VMEM((4, features, columns), BF16),
            pltpu.VMEM((rows, features), BF16),
            pltpu.VMEM((4, rows, columns), BF16),
            pltpu.SemaphoreType.DMA((5,)),
            pltpu.SemaphoreType.DMA((4,)),
            pltpu.SemaphoreType.DMA((4,)),
        ],
    )(blocks, q, *weights, w_out)


def later_products(blocks, rows, w_out, heads):
    features = rows.shape[1]
    columns = w_out.shape[1] // heads
    pair = jax.ShapeDtypeStruct((2, rows.shape[0], columns), BF16)
    return pl.pallas_call(
        later_products_kernel,
        out_shape=(pair, pair),
        in_specs=[SMEM] + [ANY] * 2,
        out_specs=(ANY,) * 2,
        scratch_shapes=[
            pltpu.VMEM((4, features, columns), BF16),
            pltpu.VMEM(rows.shape, BF16),
            pltpu.VMEM((4, rows.shape[0], columns), BF16),
            pltpu.SemaphoreType.DMA,
            pltpu.SemaphoreType.DMA((4,)),
            pltpu.SemaphoreType.DMA((4,)),
        ],
    )(blocks, rows, w_out)


def halve_kernel(a_ref, ar_ref, b_ref, br_ref, a_keep, a_send, b_keep, b_send):
    for kept, come, keep, send in ((a_ref, ar_ref, a_keep, a_send), (b_ref, br_ref, b_keep, b_send)):
        keep[...] = (kept[0].astype(F32) + come[0].astype(F32)).astype(BF16)
        send[...] = (kept[1].astype(F32) + come[1].astype(F32)).astype(BF16)


def halve(a, a_come, b, b_come):
    shape = jax.ShapeDtypeStruct(a.shape[1:], BF16)
    return call(halve_kernel, (shape,) * 4, (a, a_come, b, b_come))


def choose_kernel(far_ref, a_ref, ar_ref, b_ref, br_ref, keep_ref, send_ref):
    a = (a_ref[...].astype(F32) + ar_ref[...].astype(F32)).astype(BF16)
    b = (b_ref[...].astype(F32) + br_ref[...].astype(F32)).astype(BF16)
    second = far_ref[0] == 1
    keep_ref[...] = jnp.where(second, b, a)
    send_ref[...] = jnp.where(second, a, b)


def choose(far, a, a_come, b, b_come):
    shape = jax.ShapeDtypeStruct(a.shape, BF16)
    return call(choose_kernel, (shape, shape), (far, a, a_come, b, b_come), smem=1)


def attend_kernel(position_ref, q_ref, k_ref, v_ref, kp_ref, vp_ref, out_ref):
    rows = q_ref.shape[0]
    has_prior = position_ref[0] > 0
    row = lax.broadcasted_iota(jnp.int32, (rows, rows), 0)
    column = lax.broadcasted_iota(jnp.int32, (rows, rows), 1)
    here = column <= row
    for h in range(q_ref.shape[1] // AD):
        cols = slice(h * AD, (h + 1) * AD)
        q = q_ref[:, cols]
        now = nt(q, k_ref[:, cols])
        before = nt(q, kp_ref[:, cols])
        before = jnp.where(has_prior, before * AD**-0.5, -1e30)
        scores = jnp.where(here, now * AD**-0.5, before)
        e = jnp.exp(scores - jnp.max(scores, axis=-1, keepdims=True))
        probs = e / jnp.sum(e, axis=-1, keepdims=True)
        probs_now = jnp.where(here, probs, 0.0).astype(BF16)
        probs_before = jnp.where(here, 0.0, probs).astype(BF16)
        out_ref[:, cols] = nn(probs_now, v_ref[:, cols]) + nn(probs_before, vp_ref[:, cols])


def attend(position, q, k, v, k_prior, v_prior):
    return call(
        attend_kernel, jax.ShapeDtypeStruct(q.shape, F32), (position, q, k, v, k_prior, v_prior), smem=1
    )


def swap(x, axis):
    return lax.ppermute(x, axis, [(0, 1), (1, 0)])


def half_sum(own, come):
    return (own.astype(F32) + come.astype(F32)).astype(BF16)


def block_sum(half):
    arrived = lax.all_to_all(half, CHIPS, 0, 0, tiled=True)
    return arrived.astype(F32).sum(axis=0).astype(BF16)


def from_every_chip(share):
    copies = jnp.broadcast_to(share, (lax.axis_size(CHIPS), *share.shape))
    return lax.all_to_all(copies, CHIPS, 0, 0, tiled=True)


def near(x):
    return pltpu.with_memory_space_constraint(x, pltpu.VMEM)


def together(*arrays):
    return lax.optimization_barrier(arrays)


def flip(x, mask):
    devices = range(lax.axis_size(HEAD[1]))
    return lax.ppermute(x, HEAD[1], [(i, i ^ mask) for i in devices])


def on_device(fast_q, fast_k, fast_v, rates, w_gate, w_up, w_down, w_out, att_q, att_k, att_v):
    chips = lax.axis_size(CHIPS)
    heads = lax.axis_size(HEAD)
    core = lax.axis_index("core").astype(jnp.int32).reshape(1)
    seat = lax.axis_index(SEQ[1:]).astype(jnp.int32).reshape(1)
    span = lax.axis_index("span")
    position = lax.axis_index(SEQ).astype(jnp.int32).reshape(1)
    seats = lax.axis_size(SEQ)
    far = lax.axis_index(HEAD[0]).astype(jnp.int32).reshape(1)
    x = lax.axis_index(HEAD[1]).astype(jnp.int32)
    line = lax.axis_size(HEAD[1])
    weights = (w_gate, w_up, w_down)

    route = [(i, i + 1) for i in range(seats - 1)]
    k_prior = lax.ppermute(att_k, SEQ, route)
    v_prior = lax.ppermute(att_v, SEQ, route)

    own, away = gradients(core, fast_k, fast_v, rates, weights, chips)
    share = block_sum(half_sum(own, swap(away, "core")))
    given = lax.ppermute(share, "span", [(0, 1)])
    k_prior, v_prior, share = together(k_prior, v_prior, share)
    attended = attend(position, att_q, att_k, att_v, near(k_prior), near(v_prior))
    given, attended = together(given, attended)
    own = from_every_chip(given)
    weights, own, away = update(core, rates, near(own), near(swap(own, "core")), weights, fast_k, fast_v)

    sent = jnp.stack([x ^ 1, x ^ 2, line + (x ^ 3), line + (x ^ 2)])
    held = jnp.stack([x, x ^ 3, line + x, line + (x ^ 1)])
    come = swap(away, "core")
    a_sent, b_sent, rows = first_products(sent, fast_q, weights, w_out, heads)
    come, a_sent, b_sent, rows = together(come, a_sent, b_sent, rows)
    a_come = flip(a_sent, 1)
    b_come = flip(b_sent, 3)
    a_held, b_held = later_products(held, rows, w_out, heads)
    share = block_sum(half_sum(own, come))
    share, a_held, b_held = together(share, a_held, b_held)
    a_held, a_sent, b_held, b_sent = halve(a_held, near(a_come), b_held, near(b_come))
    a_come = flip(a_sent, 3)
    b_come = flip(b_sent, 1)
    own = from_every_chip(share)
    own, a_sent, b_sent = together(own, a_sent, b_sent)
    away = swap(own, "core")
    held, sent = choose(far, a_held, near(a_come), b_held, near(b_come))
    come = swap(sent, HEAD[0])

    mine, peer = last_update(core, seat, near(own), near(away), weights, w_gate.shape[1] // seats)
    given = lax.ppermute(peer, "span", [(1, 0)])
    final = jnp.where(span == 1, mine, given)[:, None]
    mixed = (attended + held.astype(F32) + come.astype(F32)).astype(BF16)
    return mixed, final


def solution(mesh):
    split = Mesh(mesh.devices.reshape(2, 2, 4, 2, 2, 4), (*SEQ, *HEAD))
    in_specs = (
        P(SEQ, HEAD),
        P(SEQ, HEAD),
        P(SEQ, HEAD),
        P(HEAD, SEQ),
        P(HEAD, None, None),
        P(HEAD, None, None),
        P(HEAD, None, None),
        P(HEAD, None),
        P(SEQ, HEAD),
        P(SEQ, HEAD),
        P(SEQ, HEAD),
    )
    out_specs = (P(SEQ, HEAD), P(None, HEAD, SEQ, None))
    return jax.shard_map(on_device, mesh=split, in_specs=in_specs, out_specs=out_specs, check_vma=False)
```

profile of v0, /device:TPU:8, one launch (start us, length us, event | category | flops | bytes accessed | tf_op | source)
XLA Modules:
  0.0 162.9 jit_solution(6271531629675788099)
XLA Ops:
  0.6 5.5 %shard_map.122 = (bf16[8,3,32,512]{3,2,1,0:T(8,128)(2,1)}, bf16[8,3,32,512]{3,2,1,0:T(8,128)(2,1)}) custom-call(s32[1]{0:T(128)} %bitcast.core_ref, f32[1,256]{1,0:T(1,128)} %rate_ref.3, bf16[256,512]{1,0:T(8,128)(2,1)} %k_in.3, bf16[256,512]{1,0:T(8,128)(2,1)} %v_in.3, bf16[1,512,512]{2,1,0:T(8,128)(2,1)} %wg_in.3, bf16[1,512,512]{2,1,0:T(8,128)(2,1)} %wu_in.3, ...), custom_call_target="tpu_custom_call" | custom-call | tf_op jit(solution)/shard_map/pallas_call | solution.py:130
  6.2 0.1 collective-permute-start
  6.3 2.5 %collective-permute-done = bf16[8,3,32,512]{3,2,1,0:T(8,128)(2,1)S(1)} collective-permute-done((bf16[8,3,32,512]{3,2,1,0:T(8,128)(2,1)}, bf16[8,3,32,512]{3,2,1,0:T(8,128)(2,1)S(1)}, u32[]{:S(2)}, u32[]{:S(2)}) %collective-permute-start) | collective-permute-done | bytes 786464 | tf_op jit(solution)/shard_map/ppermute | solution.py:413
  8.8 0.0 copy-start.2
  8.8 2.4 %add_convert_fusion.1 = bf16[8,3,32,512]{3,2,1,0:T(8,128)(2,1)} fusion(bf16[8,3,32,512]{3,2,1,0:T(8,128)(2,1)S(1)} %collective-permute-done, bf16[8,3,32,512]{3,2,1,0:T(8,128)(2,1)} %get-tuple-element.34), kind=kLoop, calls=%fused_computation.1 | loop fusion | flops 1572864 | bytes 2359296 | tf_op jit(solution)/shard_map/convert_element_type | solution.py:417
  11.2 6.3 %all-to-all-start = ((bf16[8,3,32,512]{3,2,1,0:T(8,128)(2,1)}), bf16[8,3,32,512]{3,2,1,0:T(8,128)(2,1)S(1)}, u32[]{:S(2)}, u32[]{:S(2)}) async-start(bf16[8,3,32,512]{3,2,1,0:T(8,128)(2,1)} %add_convert_fusion.1), calls=%async_computation | async-start | bytes 1572864 | tf_op jit(solution)/shard_map/all_to_all | solution.py:421
  17.4 0.0 copy-done.2
  17.4 1.9 %collective-permute-start.2 = (bf16[256,640]{1,0:T(8,128)(2,1)S(1)}, bf16[256,640]{1,0:T(8,128)(2,1)S(1)}, u32[]{:S(2)}, u32[]{:S(2)}) collective-permute-start(bf16[256,640]{1,0:T(8,128)(2,1)S(1)} %copy-done.2), channel_id=1, source_target_pairs={{0,8},{8,16},{16,24},{24,32},{32,40},{40,48},{48,56},{56,64},{64,7... | collective-permute-start | bytes 983048 | tf_op jit(solution)/shard_map/ppermute | solution.py:457
  19.4 0.0 copy-done.3
  19.4 3.5 %collective-permute-start.3 = (bf16[256,640]{1,0:T(8,128)(2,1)S(1)}, bf16[256,640]{1,0:T(8,128)(2,1)S(1)}, u32[]{:S(2)}, u32[]{:S(2)}) collective-permute-start(bf16[256,640]{1,0:T(8,128)(2,1)S(1)} %copy-done.3), channel_id=1, source_target_pairs={{0,8},{8,16},{16,24},{24,32},{32,40},{40,48},{48,56},{56,64},{64,7... | collective-permute-start | bytes 983048 | tf_op jit(solution)/shard_map/ppermute | solution.py:458
  22.9 5.7 %all-to-all-done = bf16[8,3,32,512]{3,2,1,0:T(8,128)(2,1)S(1)} async-done(((bf16[8,3,32,512]{3,2,1,0:T(8,128)(2,1)}), bf16[8,3,32,512]{3,2,1,0:T(8,128)(2,1)S(1)}, u32[]{:S(2)}, u32[]{:S(2)}) %all-to-all-start) | async-done | bytes 786464 | tf_op jit(solution)/shard_map/all_to_all | solution.py:421
  28.6 0.1 reduce_sum.24
  28.7 5.2 %collective-permute-start.1 = (bf16[3,32,512]{2,1,0:T(8,128)(2,1)S(1)}, bf16[3,32,512]{2,1,0:T(8,128)(2,1)S(1)}, u32[]{:S(2)}, u32[]{:S(2)}) collective-permute-start(bf16[3,32,512]{2,1,0:T(8,128)(2,1)S(1)} %reduce_sum.24), channel_id=1, source_target_pairs={{0,128},{1,129},{2,130},{3,131},{4,132},{5,133},{6,134},{7,135},{8... | collective-permute-start | bytes 294920 | tf_op jit(solution)/shard_map/ppermute | solution.py:462
  33.9 0.0 collective-permute-done.2.kp_ref
  33.9 0.0 collective-permute-done.3.vp_ref
  33.9 4.2 %shard_map.123 = f32[256,640]{1,0:T(8,128)} custom-call(s32[1]{0:T(128)} %bitcast.1.position_ref, bf16[256,640]{1,0:T(8,128)(2,1)} %q_ref.1, bf16[256,640]{1,0:T(8,128)(2,1)} %k_ref.1, bf16[256,640]{1,0:T(8,128)(2,1)} %v_ref.1, bf16[256,640]{1,0:T(8,128)(2,1)S(1)} %collective-permute-done.2.kp_ref, bf16[256,640]{1,0:T(8,128)(2,1)S(1)} %collective-permute-done.3.vp_ref), custom_call_target="tpu_custom_call" | custom-call | tf_op jit(solution)/shard_map/pallas_call | solution.py:37
  38.1 0.0 collective-permute-done.1
  38.1 0.1 broadcast_in_dim.9
  38.2 21.6 %all_to_all.20.own_in = bf16[8,3,32,512]{3,2,1,0:T(8,128)(2,1)S(1)} all-to-all(bf16[8,3,32,512]{3,2,1,0:T(8,128)(2,1)S(1)} %broadcast_in_dim.9), channel_id=1, replica_groups=mesh['span'=2,'row'=2,'y'=4,'core'=2,'head_0'=2,'head_1'=4] {'row','y'}, dimensions={0} | all-to-all | bytes 1572864 | tf_op jit(solution)/shard_map/all_to_all | solution.py:427
  59.8 0.0 collective-permute-start.4
  59.8 2.3 %collective-permute-done.4.far_in = bf16[8,3,32,512]{3,2,1,0:T(8,128)(2,1)S(1)} collective-permute-done((bf16[8,3,32,512]{3,2,1,0:T(8,128)(2,1)S(1)}, bf16[8,3,32,512]{3,2,1,0:T(8,128)(2,1)S(1)}, u32[]{:S(2)}, u32[]{:S(2)}) %collective-permute-start.4) | collective-permute-done | bytes 786464 | tf_op jit(solution)/shard_map/ppermute | solution.py:413
  62.1 11.4 %shard_map.124 = (bf16[1,512,512]{2,1,0:T(8,128)(2,1)}, bf16[1,512,512]{2,1,0:T(8,128)(2,1)}, bf16[1,512,512]{2,1,0:T(8,128)(2,1)}, bf16[8,3,32,512]{3,2,1,0:T(8,128)(2,1)}, bf16[8,3,32,512]{3,2,1,0:T(8,128)(2,1)}) custom-call(s32[1]{0:T(128)} %bitcast.core_ref, f32[1,256]{1,0:T(1,128)} %rate_ref.3, bf16[8,3,32,512]{3,2,1,0:T(8,128)(2,1)S(1)} %all_to_all.20.own_in, ...), custom_call_target="tpu_custom_call" | custom-call | tf_op jit(solution)/shard_map/pallas_call | solution.py:217
  73.6 0.2 collective-permute-start.5
  73.8 0.6 pad_add_fusion.blocks_ref
  74.4 0.0 copy-start.1
  74.4 5.9 %shard_map.125 = (bf16[2,256,640]{2,1,0:T(8,128)(2,1)}, bf16[2,256,640]{2,1,0:T(8,128)(2,1)}, bf16[256,512]{1,0:T(8,128)(2,1)}) custom-call(s32[4]{0:T(128)} %pad_add_fusion.blocks_ref, bf16[256,512]{1,0:T(8,128)(2,1)} %q_in.1, bf16[1,512,512]{2,1,0:T(8,128)(2,1)} %get-tuple-element.42.wg_in, bf16[1,512,512]{2,1,0:T(8,128)(2,1)} %get-tuple-element.43.wu_in, ...), custom_call_target="tpu_custom_call" | custom-call | tf_op jit(solution)/shard_map/pallas_call | solution.py:324
  80.3 0.0 collective-permute-done.5
  80.3 0.0 copy-done.1
  80.3 1.2 add_convert_fusion
  81.5 5.3 %all-to-all-start.2 = ((bf16[8,3,32,512]{3,2,1,0:T(8,128)(2,1)}), bf16[8,3,32,512]{3,2,1,0:T(8,128)(2,1)S(1)}, u32[]{:S(2)}, u32[]{:S(2)}) async-start(bf16[8,3,32,512]{3,2,1,0:T(8,128)(2,1)} %add_convert_fusion), calls=%async_computation.2 | async-start | bytes 1572864 | tf_op jit(solution)/shard_map/all_to_all | solution.py:421
  86.8 0.6 pad_add_fusion.1.blocks_ref
  87.4 4.5 %shard_map.126 = (bf16[2,256,640]{2,1,0:T(8,128)(2,1)}, bf16[2,256,640]{2,1,0:T(8,128)(2,1)}) custom-call(s32[4]{0:T(128)} %pad_add_fusion.1.blocks_ref, bf16[256,512]{1,0:T(8,128)(2,1)} %get-tuple-element.49.rows_in, bf16[512,5120]{1,0:T(8,128)(2,1)} %wo_in.3), custom_call_target="tpu_custom_call" | custom-call | tf_op jit(solution)/shard_map/pallas_call | solution.py:346
  91.9 0.0 copy-start.7
  91.9 0.0 copy-start.6
  91.9 6.5 %all-to-all-done.2 = bf16[8,3,32,512]{3,2,1,0:T(8,128)(2,1)S(1)} async-done(((bf16[8,3,32,512]{3,2,1,0:T(8,128)(2,1)}), bf16[8,3,32,512]{3,2,1,0:T(8,128)(2,1)S(1)}, u32[]{:S(2)}, u32[]{:S(2)}) %all-to-all-start.2) | async-done | bytes 786464 | tf_op jit(solution)/shard_map/all_to_all | solution.py:421
  98.4 0.1 reduce_sum.25
  98.5 1.0 broadcast_in_dim.10
  99.5 4.8 %all-to-all-start.3 = ((bf16[8,3,32,512]{3,2,1,0:T(8,128)(2,1)}), bf16[8,3,32,512]{3,2,1,0:T(8,128)(2,1)S(1)}, u32[]{:S(2)}, u32[]{:S(2)}) async-start(bf16[8,3,32,512]{3,2,1,0:T(8,128)(2,1)} %broadcast_in_dim.10), calls=%async_computation.3 | async-start | bytes 1572864 | tf_op jit(solution)/shard_map/all_to_all | solution.py:427
  104.3 0.0 copy-done.7
  104.3 1.5 collective-permute-start.6
  105.8 0.0 copy-done.6
  105.8 2.1 %collective-permute-start.7 = (bf16[2,256,640]{2,1,0:T(8,128)(2,1)S(1)}, bf16[2,256,640]{2,1,0:T(8,128)(2,1)S(1)}, u32[]{:S(2)}, u32[]{:S(2)}) collective-permute-start(bf16[2,256,640]{2,1,0:T(8,128)(2,1)S(1)} %copy-done.6), channel_id=1, source_target_pairs={{0,3},{1,2},{2,1},{3,0},{4,7},{5,6},{6,5},{7,4},{8,11},{9,10},{10,... | collective-permute-start | bytes 1966088 | tf_op jit(solution)/shard_map/ppermute | solution.py:440
  107.9 12.5 %collective-permute-done.6.ar_ref = bf16[2,256,640]{2,1,0:T(8,128)(2,1)S(1)} collective-permute-done((bf16[2,256,640]{2,1,0:T(8,128)(2,1)S(1)}, bf16[2,256,640]{2,1,0:T(8,128)(2,1)S(1)}, u32[]{:S(2)}, u32[]{:S(2)}) %collective-permute-start.6) | collective-permute-done | bytes 655392 | tf_op jit(solution)/shard_map/ppermute | solution.py:440
  120.4 2.4 %collective-permute-done.7.br_ref = bf16[2,256,640]{2,1,0:T(8,128)(2,1)S(1)} collective-permute-done((bf16[2,256,640]{2,1,0:T(8,128)(2,1)S(1)}, bf16[2,256,640]{2,1,0:T(8,128)(2,1)S(1)}, u32[]{:S(2)}, u32[]{:S(2)}) %collective-permute-start.7) | collective-permute-done | bytes 655392 | tf_op jit(solution)/shard_map/ppermute | solution.py:440
  122.9 2.4 %shard_map.127 = (bf16[256,640]{1,0:T(8,128)(2,1)}, bf16[256,640]{1,0:T(8,128)(2,1)}, bf16[256,640]{1,0:T(8,128)(2,1)}, bf16[256,640]{1,0:T(8,128)(2,1)}) custom-call(bf16[2,256,640]{2,1,0:T(8,128)(2,1)} %get-tuple-element.52.a_ref, bf16[2,256,640]{2,1,0:T(8,128)(2,1)S(1)} %collective-permute-done.6.ar_ref, bf16[2,256,640]{2,1,0:T(8,128)(2,1)} %get-tuple-element.54.b_ref, ...), custom_call_target="tpu_custom_call" | custom-call | tf_op jit(solution)/shard_map/pallas_call | solution.py:37
  125.3 0.0 all-to-all-done.3.own_in
  125.3 0.0 collective-permute-start.11
  125.3 2.2 %collective-permute-start.8 = (bf16[256,640]{1,0:T(8,128)(2,1)}, bf16[256,640]{1,0:T(8,128)(2,1)S(1)}, u32[]{:S(2)}, u32[]{:S(2)}) collective-permute-start(bf16[256,640]{1,0:T(8,128)(2,1)} %get-tuple-element.57), channel_id=1, source_target_pairs={{0,3},{1,2},{2,1},{3,0},{4,7},{5,6},{6,5},{7,4},{8,11},{9,10},{10,... | collective-permute-start | bytes 983048 | tf_op jit(solution)/shard_map/ppermute | solution.py:440
  127.5 0.0 collective-permute-start.9
  127.5 9.4 %collective-permute-done.8.ar_ref = bf16[256,640]{1,0:T(8,128)(2,1)S(1)} collective-permute-done((bf16[256,640]{1,0:T(8,128)(2,1)}, bf16[256,640]{1,0:T(8,128)(2,1)S(1)}, u32[]{:S(2)}, u32[]{:S(2)}) %collective-permute-start.8) | collective-permute-done | bytes 327712 | tf_op jit(solution)/shard_map/ppermute | solution.py:440
  136.8 0.6 collective-permute-done.9.br_ref
  137.4 2.1 %shard_map.128 = (bf16[256,640]{1,0:T(8,128)(2,1)}, bf16[256,640]{1,0:T(8,128)(2,1)}) custom-call(s32[1]{0:T(128)} %bitcast.2.far_ref, bf16[256,640]{1,0:T(8,128)(2,1)} %get-tuple-element.56.a_ref, bf16[256,640]{1,0:T(8,128)(2,1)S(1)} %collective-permute-done.8.ar_ref, bf16[256,640]{1,0:T(8,128)(2,1)} %get-tuple-element.58.b_ref, ...), custom_call_target="tpu_custom_call" | custom-call | tf_op jit(solution)/shard_map/pallas_call | solution.py:37
  139.5 4.5 %collective-permute-start.10 = (bf16[256,640]{1,0:T(8,128)(2,1)}, bf16[256,640]{1,0:T(8,128)(2,1)S(1)}, u32[]{:S(2)}, u32[]{:S(2)}) collective-permute-start(bf16[256,640]{1,0:T(8,128)(2,1)} %get-tuple-element.61), channel_id=1, source_target_pairs={{0,4},{4,0},{1,5},{5,1},{2,6},{6,2},{3,7},{7,3},{8,12},{12,8},{9,1... | collective-permute-start | bytes 983048 | tf_op jit(solution)/shard_map/ppermute | solution.py:413
  144.0 0.0 collective-permute-done.11.far_in
  144.0 8.0 %shard_map.129 = (bf16[3,16,512]{2,1,0:T(8,128)(2,1)}, bf16[3,16,512]{2,1,0:T(8,128)(2,1)}) custom-call(s32[1]{0:T(128)} %bitcast.core_ref, s32[1]{0:T(128)} %bitcast.11.seat_ref, bf16[8,3,32,512]{3,2,1,0:T(8,128)(2,1)S(1)} %all-to-all-done.3.own_in, bf16[8,3,32,512]{3,2,1,0:T(8,128)(2,1)S(1)} %collective-permute-done.11.far_in, ...), custom_call_target="tpu_custom_call" | custom-call | tf_op jit(solution)/shard_map/pallas_call | solution.py:257
  152.1 0.0 copy-start.5
  152.1 1.4 collective-permute-start.12
  153.5 6.2 %collective-permute-done.10 = bf16[256,640]{1,0:T(8,128)(2,1)S(1)} collective-permute-done((bf16[256,640]{1,0:T(8,128)(2,1)}, bf16[256,640]{1,0:T(8,128)(2,1)S(1)}, u32[]{:S(2)}, u32[]{:S(2)}) %collective-permute-start.10) | collective-permute-done | bytes 327712 | tf_op jit(solution)/shard_map/ppermute | solution.py:413
  159.7 0.0 copy-done
  159.7 0.0 copy-done.4
  159.7 0.8 add_convert_fusion.2
  160.5 1.8 %collective-permute-done.12 = bf16[3,16,512]{2,1,0:T(8,128)(2,1)S(1)} collective-permute-done((bf16[3,16,512]{2,1,0:T(8,128)(2,1)}, bf16[3,16,512]{2,1,0:T(8,128)(2,1)S(1)}, u32[]{:S(2)}, u32[]{:S(2)}) %collective-permute-start.12) | collective-permute-done | bytes 49184 | tf_op jit(solution)/shard_map/ppermute | solution.py:489
  162.3 0.0 copy-done.5
  162.3 0.6 select_bitcast_fusion
  (3 shorter events, 0.0 us)
Async XLA Ops:
  6.2 2.6 %collective-permute-start = (bf16[8,3,32,512]{3,2,1,0:T(8,128)(2,1)}, bf16[8,3,32,512]{3,2,1,0:T(8,128)(2,1)S(1)}, u32[]{:S(2)}, u32[]{:S(2)}) collective-permute-start(bf16[8,3,32,512]{3,2,1,0:T(8,128)(2,1)} %get-tuple-element.35), channel_id=1, source_target_pairs={{0,8},{8,0},{1,9},{9,1},{2,10},{10,2},{3,11},{11,3},{4,12},{12,4},... | collective-permute-start | bytes 2359304 | tf_op jit(solution)/shard_map/ppermute | solution.py:413
  8.8 8.7 %copy-start.2 = (bf16[256,640]{1,0:T(8,128)(2,1)S(1)}, bf16[256,640]{1,0:T(8,128)(2,1)}, u32[]{:S(2)}) copy-start(bf16[256,640]{1,0:T(8,128)(2,1)} %k_ref.1) | copy-start | bytes 983044
  8.8 10.6 %copy-start.3 = (bf16[256,640]{1,0:T(8,128)(2,1)S(1)}, bf16[256,640]{1,0:T(8,128)(2,1)}, u32[]{:S(2)}) copy-start(bf16[256,640]{1,0:T(8,128)(2,1)} %v_ref.1) | copy-start | bytes 983044
  11.2 17.4 %all-to-all-start = ((bf16[8,3,32,512]{3,2,1,0:T(8,128)(2,1)}), bf16[8,3,32,512]{3,2,1,0:T(8,128)(2,1)S(1)}, u32[]{:S(2)}, u32[]{:S(2)}) async-start(bf16[8,3,32,512]{3,2,1,0:T(8,128)(2,1)} %add_convert_fusion.1), calls=%async_computation | async-start | bytes 1572864 | tf_op jit(solution)/shard_map/all_to_all | solution.py:421
  17.4 16.4 %collective-permute-start.2 = (bf16[256,640]{1,0:T(8,128)(2,1)S(1)}, bf16[256,640]{1,0:T(8,128)(2,1)S(1)}, u32[]{:S(2)}, u32[]{:S(2)}) collective-permute-start(bf16[256,640]{1,0:T(8,128)(2,1)S(1)} %copy-done.2), channel_id=1, source_target_pairs={{0,8},{8,16},{16,24},{24,32},{32,40},{40,48},{48,56},{56,64},{64,7... | collective-permute-start | bytes 983048 | tf_op jit(solution)/shard_map/ppermute | solution.py:457
  19.4 14.5 %collective-permute-start.3 = (bf16[256,640]{1,0:T(8,128)(2,1)S(1)}, bf16[256,640]{1,0:T(8,128)(2,1)S(1)}, u32[]{:S(2)}, u32[]{:S(2)}) collective-permute-start(bf16[256,640]{1,0:T(8,128)(2,1)S(1)} %copy-done.3), channel_id=1, source_target_pairs={{0,8},{8,16},{16,24},{24,32},{32,40},{40,48},{48,56},{56,64},{64,7... | collective-permute-start | bytes 983048 | tf_op jit(solution)/shard_map/ppermute | solution.py:458
  28.7 9.4 %collective-permute-start.1 = (bf16[3,32,512]{2,1,0:T(8,128)(2,1)S(1)}, bf16[3,32,512]{2,1,0:T(8,128)(2,1)S(1)}, u32[]{:S(2)}, u32[]{:S(2)}) collective-permute-start(bf16[3,32,512]{2,1,0:T(8,128)(2,1)S(1)} %reduce_sum.24), channel_id=1, source_target_pairs={{0,128},{1,129},{2,130},{3,131},{4,132},{5,133},{6,134},{7,135},{8... | collective-permute-start | bytes 294920 | tf_op jit(solution)/shard_map/ppermute | solution.py:462
  59.8 2.3 %collective-permute-start.4 = (bf16[8,3,32,512]{3,2,1,0:T(8,128)(2,1)S(1)}, bf16[8,3,32,512]{3,2,1,0:T(8,128)(2,1)S(1)}, u32[]{:S(2)}, u32[]{:S(2)}) collective-permute-start(bf16[8,3,32,512]{3,2,1,0:T(8,128)(2,1)S(1)} %all_to_all.20.own_in), channel_id=1, source_target_pairs={{0,8},{8,0},{1,9},{9,1},{2,10},{10,2},{3,11},{11,3},{4,12},{12,4},... | collective-permute-start | bytes 2359304 | tf_op jit(solution)/shard_map/ppermute | solution.py:413
  73.6 6.7 %collective-permute-start.5 = (bf16[8,3,32,512]{3,2,1,0:T(8,128)(2,1)}, bf16[8,3,32,512]{3,2,1,0:T(8,128)(2,1)S(1)}, u32[]{:S(2)}, u32[]{:S(2)}) collective-permute-start(bf16[8,3,32,512]{3,2,1,0:T(8,128)(2,1)} %get-tuple-element.41), channel_id=1, source_target_pairs={{0,8},{8,0},{1,9},{9,1},{2,10},{10,2},{3,11},{11,3},{4,12},{12,4},... | collective-permute-start | bytes 2359304 | tf_op jit(solution)/shard_map/ppermute | solution.py:413
  74.4 5.9 %copy-start.1 = (bf16[8,3,32,512]{3,2,1,0:T(8,128)(2,1)S(1)}, bf16[8,3,32,512]{3,2,1,0:T(8,128)(2,1)}, u32[]{:S(2)}) copy-start(bf16[8,3,32,512]{3,2,1,0:T(8,128)(2,1)} %get-tuple-element.40) | copy-start | bytes 2359300
  81.5 16.9 %all-to-all-start.2 = ((bf16[8,3,32,512]{3,2,1,0:T(8,128)(2,1)}), bf16[8,3,32,512]{3,2,1,0:T(8,128)(2,1)S(1)}, u32[]{:S(2)}, u32[]{:S(2)}) async-start(bf16[8,3,32,512]{3,2,1,0:T(8,128)(2,1)} %add_convert_fusion), calls=%async_computation.2 | async-start | bytes 1572864 | tf_op jit(solution)/shard_map/all_to_all | solution.py:421
  91.9 12.4 %copy-start.7 = (bf16[2,256,640]{2,1,0:T(8,128)(2,1)S(1)}, bf16[2,256,640]{2,1,0:T(8,128)(2,1)}, u32[]{:S(2)}) copy-start(bf16[2,256,640]{2,1,0:T(8,128)(2,1)} %get-tuple-element.53) | copy-start | bytes 1966084
  91.9 13.9 %copy-start.6 = (bf16[2,256,640]{2,1,0:T(8,128)(2,1)S(1)}, bf16[2,256,640]{2,1,0:T(8,128)(2,1)}, u32[]{:S(2)}) copy-start(bf16[2,256,640]{2,1,0:T(8,128)(2,1)} %get-tuple-element.55) | copy-start | bytes 1966084
  99.5 25.8 %all-to-all-start.3 = ((bf16[8,3,32,512]{3,2,1,0:T(8,128)(2,1)}), bf16[8,3,32,512]{3,2,1,0:T(8,128)(2,1)S(1)}, u32[]{:S(2)}, u32[]{:S(2)}) async-start(bf16[8,3,32,512]{3,2,1,0:T(8,128)(2,1)} %broadcast_in_dim.10), calls=%async_computation.3 | async-start | bytes 1572864 | tf_op jit(solution)/shard_map/all_to_all | solution.py:427
  104.3 16.1 %collective-permute-start.6 = (bf16[2,256,640]{2,1,0:T(8,128)(2,1)S(1)}, bf16[2,256,640]{2,1,0:T(8,128)(2,1)S(1)}, u32[]{:S(2)}, u32[]{:S(2)}) collective-permute-start(bf16[2,256,640]{2,1,0:T(8,128)(2,1)S(1)} %copy-done.7), channel_id=1, source_target_pairs={{0,1},{1,0},{2,3},{3,2},{4,5},{5,4},{6,7},{7,6},{8,9},{9,8},{10,11... | collective-permute-start | bytes 1966088 | tf_op jit(solution)/shard_map/ppermute | solution.py:440
  105.8 17.1 %collective-permute-start.7 = (bf16[2,256,640]{2,1,0:T(8,128)(2,1)S(1)}, bf16[2,256,640]{2,1,0:T(8,128)(2,1)S(1)}, u32[]{:S(2)}, u32[]{:S(2)}) collective-permute-start(bf16[2,256,640]{2,1,0:T(8,128)(2,1)S(1)} %copy-done.6), channel_id=1, source_target_pairs={{0,3},{1,2},{2,1},{3,0},{4,7},{5,6},{6,5},{7,4},{8,11},{9,10},{10,... | collective-permute-start | bytes 1966088 | tf_op jit(solution)/shard_map/ppermute | solution.py:440
  125.3 18.7 %collective-permute-start.11 = (bf16[8,3,32,512]{3,2,1,0:T(8,128)(2,1)S(1)}, bf16[8,3,32,512]{3,2,1,0:T(8,128)(2,1)S(1)}, u32[]{:S(2)}, u32[]{:S(2)}) collective-permute-start(bf16[8,3,32,512]{3,2,1,0:T(8,128)(2,1)S(1)} %all-to-all-done.3.own_in), channel_id=1, source_target_pairs={{0,8},{8,0},{1,9},{9,1},{2,10},{10,2},{3,11},{11,3},{4,12},{12,4},... | collective-permute-start | bytes 2359304 | tf_op jit(solution)/shard_map/ppermute | solution.py:413
  125.3 11.5 %collective-permute-start.8 = (bf16[256,640]{1,0:T(8,128)(2,1)}, bf16[256,640]{1,0:T(8,128)(2,1)S(1)}, u32[]{:S(2)}, u32[]{:S(2)}) collective-permute-start(bf16[256,640]{1,0:T(8,128)(2,1)} %get-tuple-element.57), channel_id=1, source_target_pairs={{0,3},{1,2},{2,1},{3,0},{4,7},{5,6},{6,5},{7,4},{8,11},{9,10},{10,... | collective-permute-start | bytes 983048 | tf_op jit(solution)/shard_map/ppermute | solution.py:440
  127.5 10.0 %collective-permute-start.9 = (bf16[256,640]{1,0:T(8,128)(2,1)}, bf16[256,640]{1,0:T(8,128)(2,1)S(1)}, u32[]{:S(2)}, u32[]{:S(2)}) collective-permute-start(bf16[256,640]{1,0:T(8,128)(2,1)} %get-tuple-element.59), channel_id=1, source_target_pairs={{0,1},{1,0},{2,3},{3,2},{4,5},{5,4},{6,7},{7,6},{8,9},{9,8},{10,11... | collective-permute-start | bytes 983048 | tf_op jit(solution)/shard_map/ppermute | solution.py:440
  139.5 20.1 %collective-permute-start.10 = (bf16[256,640]{1,0:T(8,128)(2,1)}, bf16[256,640]{1,0:T(8,128)(2,1)S(1)}, u32[]{:S(2)}, u32[]{:S(2)}) collective-permute-start(bf16[256,640]{1,0:T(8,128)(2,1)} %get-tuple-element.61), channel_id=1, source_target_pairs={{0,4},{4,0},{1,5},{5,1},{2,6},{6,2},{3,7},{7,3},{8,12},{12,8},{9,1... | collective-permute-start | bytes 983048 | tf_op jit(solution)/shard_map/ppermute | solution.py:413
  144.0 15.6 %copy-start = (f32[256,640]{1,0:T(8,128)S(1)}, f32[256,640]{1,0:T(8,128)}, u32[]{:S(2)}) copy-start(f32[256,640]{1,0:T(8,128)} %shard_map.123) | copy-start | bytes 1966084
  144.0 15.6 %copy-start.4 = (bf16[256,640]{1,0:T(8,128)(2,1)S(1)}, bf16[256,640]{1,0:T(8,128)(2,1)}, u32[]{:S(2)}) copy-start(bf16[256,640]{1,0:T(8,128)(2,1)} %get-tuple-element.60) | copy-start | bytes 983044
  152.1 10.2 %copy-start.5 = (bf16[3,16,512]{2,1,0:T(8,128)(2,1)S(1)}, bf16[3,16,512]{2,1,0:T(8,128)(2,1)}, u32[]{:S(2)}) copy-start(bf16[3,16,512]{2,1,0:T(8,128)(2,1)} %get-tuple-element.64) | copy-start | bytes 147460
  152.1 10.2 %collective-permute-start.12 = (bf16[3,16,512]{2,1,0:T(8,128)(2,1)}, bf16[3,16,512]{2,1,0:T(8,128)(2,1)S(1)}, u32[]{:S(2)}, u32[]{:S(2)}) collective-permute-start(bf16[3,16,512]{2,1,0:T(8,128)(2,1)} %get-tuple-element.65), channel_id=1, source_target_pairs={{128,0},{129,1},{130,2},{131,3},{132,4},{133,5},{134,6},{135,7},{1... | collective-permute-start | bytes 147464 | tf_op jit(solution)/shard_map/ppermute | solution.py:489
where the time goes:
time: 165 us; the launch traced here: 163 us
  waiting for transfers between devices  49.9 us (30%)
  Pallas kernels  44.2 us (27%)
  starting transfers between devices  38.9 us (24%)
  blocking collectives  21.6 us (13%)
  other arithmetic  6.46 us (4%)
    ppermute x4, waiting for transfers between devices, flip(): return lax.ppermute(x, HEAD[1], [(i, i ^ mask) for i in devices])  24.9 us
    all_to_all x1, blocking collectives, from_every_chip(): return lax.all_to_all(copies, CHIPS, 0, 0, tiled=True)  21.6 us
    all_to_all x2, waiting for transfers between devices, block_sum(): arrived = lax.all_to_all(half, CHIPS, 0, 0, tiled=True)  12.2 us
    all_to_all x2, starting transfers between devices, block_sum(): arrived = lax.all_to_all(half, CHIPS, 0, 0, tiled=True)  11.5 us
    pallas_call x1, Pallas kernels, update(): pl.pallas_call(update_kernel, out_shape=(weight,) * 3 + (split,) * 2, in_...  11.4 us
    ppermute x5, waiting for transfers between devices, swap(): return lax.ppermute(x, axis, [(0, 1), (1, 0)])  10.9 us
    pallas_call x3, Pallas kernels, call(): pl.pallas_call(kernel, out_shape=outs, in_specs=[SMEM] * smem + [VMEM] *...  8.71 us
    pallas_call x1, Pallas kernels, last_update(): pl.pallas_call(last_kernel, out_shape=(shape, shape), in_specs=[SMEM, SME...  8.02 us
  transfers between devices with their start and end apart: 16, of which 10 were waited for; matrix products, arithmetic and copies ran while one was open for 1% of the time, Pallas kernels for 17%

commit v1 on v0

v1 whole, which is shorter than its diff:
```python
import functools

import jax
import jax.numpy as jnp
from jax import lax
from jax.experimental import pallas as pl
from jax.experimental.pallas import tpu as pltpu
from jax.sharding import Mesh
from jax.sharding import PartitionSpec as P

AD = 128
NS_STEPS = 2
NEWTON_COEFFS = (3.4445, -4.775, 2.0315)
SEQ = ("span", "row", "y", "core")
CHIPS = ("row", "y")
HEAD = ("head_0", "head_1")
F32 = jnp.float32
BF16 = jnp.bfloat16


VMEM = pl.BlockSpec(memory_space=pltpu.VMEM)
SMEM = pl.BlockSpec(memory_space=pltpu.SMEM)
HBM = pl.BlockSpec(memory_space=pltpu.HBM)
ROOM = pltpu.CompilerParams(vmem_limit_bytes=20 << 20)


def nn(a, b):
    return lax.dot_general(a, b, (((1,), (0,)), ((), ())), preferred_element_type=F32)


def nt(a, b):
    return lax.dot_general(a, b, (((1,), (1,)), ((), ())), preferred_element_type=F32)


def tn(a, b):
    return lax.dot_general(a, b, (((0,), (0,)), ((), ())), preferred_element_type=F32)


def call(kernel, outs, args, scratch=(), smem=0):
    return pl.pallas_call(
        kernel,
        out_shape=outs,
        in_specs=[SMEM] * smem + [VMEM] * (len(args) - smem),
        out_specs=jax.tree.map(lambda _: VMEM, outs),
        scratch_shapes=scratch,
        compiler_params=ROOM,
    )(*args)


def start(source, target, sem):
    copy = pltpu.make_async_copy(source, target, sem)
    copy.start()
    return copy


def split_gradients(core, k, v, rate, weights, own_ref, far_ref):
    weighted = (rate * v.astype(F32)).astype(BF16)
    x = nn(k, weights[0])
    u = nn(k, weights[1])
    sig = jax.nn.sigmoid(x)
    silu = x * sig
    neg_act = (-(silu * u)).astype(BF16)

    def emit(m, left, right):
        blocks, _, step, features = own_ref.shape
        half = blocks * step
        for h in range(2):
            g = tn(left[:, h * half : (h + 1) * half], right).astype(BF16).reshape(blocks, step, features)

            @pl.when(core == h)
            def _():
                own_ref[:, m] = g

            @pl.when(core != h)
            def _():
                far_ref[:, m] = g

    emit(2, neg_act, weighted)
    back = -nt(weighted, weights[2])
    emit(1, k, (back * silu).astype(BF16))
    emit(0, k, (back * u * (sig * (1.0 + x * (1.0 - sig)))).astype(BF16))


def column(row):
    size = row.shape[1]
    eye = lax.broadcasted_iota(jnp.int32, (size, size), 0) == lax.broadcasted_iota(
        jnp.int32, (size, size), 1
    )
    return jnp.sum(jnp.where(eye, row, 0.0), axis=1, keepdims=True)


def gradients_kernel(
    core_ref, rate_in, k_in, v_in, wg_in, wu_in, wd_in, own_ref, far_ref, rate_ref, k_ref, v_ref, w_ref, sem
):
    loads = [
        start(source, target, sem.at[i])
        for i, (source, target) in enumerate(
            (
                (k_in, k_ref),
                (wg_in.at[0], w_ref.at[0]),
                (wu_in.at[0], w_ref.at[1]),
                (v_in, v_ref),
                (wd_in.at[0], w_ref.at[2]),
                (rate_in, rate_ref),
            )
        )
    ]
    for copy in loads:
        copy.wait()
    rate = column(rate_ref[...])
    weights = [w_ref[m] for m in range(3)]
    split_gradients(core_ref[0], k_ref[...], v_ref[...], rate, weights, own_ref, far_ref)


def split_shape(features, blocks):
    return (blocks, 3, features // 2 // blocks, features)


def gradients(core, k, v, rate, weights, blocks):
    rows, features = k.shape
    shape = pltpu.VMEM(split_shape(features, blocks), BF16)
    return pl.pallas_call(
        gradients_kernel,
        out_shape=(shape, shape),
        in_specs=[SMEM] + [HBM] * 6,
        out_specs=(VMEM, VMEM),
        scratch_shapes=[
            pltpu.VMEM(rate.shape, F32),
            pltpu.VMEM((rows, features), BF16),
            pltpu.VMEM((rows, features), BF16),
            pltpu.VMEM((3, features, features), BF16),
            pltpu.SemaphoreType.DMA((6,)),
        ],
        compiler_params=ROOM,
    )(core, rate, k, v, *weights)


def orthogonal(gradients):
    first, second, third = NEWTON_COEFFS
    xs = []
    for load in gradients:
        wide = load().astype(F32)
        xs.append((wide * lax.rsqrt(jnp.sum(wide * wide) + 1e-6)).astype(BF16))
    for _ in range(NS_STEPS):
        grams = [nt(x, x).astype(BF16) for x in xs]
        polys = [(second * g.astype(F32) + third * nn(g, g)).astype(BF16) for g in grams]
        xs = [(first * x.astype(F32) + nn(p, x)).astype(BF16) for p, x in zip(polys, xs)]
    return xs


def moved_weight(w, x):
    w = w.astype(F32)
    moved = w - x.astype(F32)
    target = jnp.sqrt(jnp.sum(w * w, axis=0, keepdims=True) + 1e-6)
    current = jnp.sqrt(jnp.sum(moved * moved, axis=0, keepdims=True) + 1e-6)
    return (moved * (target / current)).astype(BF16)


def gathered(core, own_in, far_in, g_ref, sem):
    loads = []

    def wanted(m, pair):
        def load():
            for copy in pair:
                copy.wait()
            return g_ref[m].reshape(g_ref.shape[4], g_ref.shape[4])

        return load

    for m in range(3):
        pair = (
            start(own_in.at[:, m], g_ref.at[m, core], sem.at[m]),
            start(far_in.at[:, m], g_ref.at[m, 1 - core], sem.at[3 + m]),
        )
        loads.append(wanted(m, pair))
    return loads


def update_kernel(
    core_ref, rate_in, own_in, far_in, wg_in, wu_in, wd_in, k_in, v_in,
    wg_ref, wu_ref, wd_ref, own_ref, far_ref, g_ref, rate_ref, w_ref, k_ref, v_ref, sem, g_sem,
):
    core = core_ref[0]
    loads = gathered(core, own_in, far_in, g_ref, g_sem)
    others = [start(w.at[0], w_ref.at[m], sem.at[m]) for m, w in enumerate((wg_in, wu_in, wd_in))]
    others += [start(k_in, k_ref, sem.at[3]), start(v_in, v_ref, sem.at[4]), start(rate_in, rate_ref, sem.at[5])]
    xs = orthogonal(loads)
    for copy in others:
        copy.wait()
    rate = column(rate_ref[...])
    weights = [moved_weight(w_ref[m], x) for m, x in enumerate(xs)]
    for w, out in zip(weights, (wg_ref, wu_ref, wd_ref)):
        out[0] = w
    split_gradients(core, k_ref[...], v_ref[...], rate, weights, own_ref, far_ref)


def update(core, rate, own, far, weights, k, v):
    rows, features = k.shape
    blocks, _, step, _ = own.shape
    weight = pltpu.VMEM(weights[0].shape, BF16)
    split = pltpu.VMEM(own.shape, BF16)
    out = pl.pallas_call(
        update_kernel,
        compiler_params=ROOM,
        out_shape=(weight,) * 3 + (split,) * 2,
        in_specs=[SMEM, HBM, VMEM, VMEM] + [HBM] * 5,
        out_specs=(VMEM,) * 5,
        scratch_shapes=[
            pltpu.VMEM((3, 2, blocks, step, features), BF16),
            pltpu.VMEM(rate.shape, F32),
            pltpu.VMEM((3, features, features), BF16),
            pltpu.VMEM((rows, features), BF16),
            pltpu.VMEM((rows, features), BF16),
            pltpu.SemaphoreType.DMA((6,)),
            pltpu.SemaphoreType.DMA((6,)),
        ],
    )(core, rate, own, far, *weights, k, v)
    return out[:3], out[3], out[4]


def last_kernel(
    core_ref, seat_ref, own_in, far_in, wg_ref, wu_ref, wd_ref, mine_ref, peer_ref, g_ref, w_ref, g_sem
):
    seat = seat_ref[0]
    loads = gathered(core_ref[0], own_in, far_in, g_ref, g_sem)
    share = mine_ref.shape[1]
    half = w_ref.shape[1] // 2
    for m, (old_ref, x) in enumerate(zip((wg_ref, wu_ref, wd_ref), orthogonal(loads))):
        w_ref[m] = moved_weight(old_ref[0], x)
        peer_ref[m] = w_ref[m, pl.ds(pl.multiple_of(seat * share, share), share), :]
        mine_ref[m] = w_ref[m, pl.ds(pl.multiple_of(half + seat * share, share), share), :]


def last_update(core, seat, own, far, weights, share):
    blocks, _, step, features = own.shape
    shape = jax.ShapeDtypeStruct((3, share, features), BF16)
    return pl.pallas_call(
        last_kernel,
        out_shape=(shape, shape),
        in_specs=[SMEM, SMEM] + [VMEM] * 5,
        out_specs=(VMEM, VMEM),
        scratch_shapes=[
            pltpu.VMEM((3, 2, blocks, step, features), BF16),
            pltpu.VMEM((3, features, features), BF16),
            pltpu.SemaphoreType.DMA((6,)),
        ],
        compiler_params=ROOM,
    )(core, seat, own, far, *weights)


def blocks_of(place, wo_in, wo_ref, sem):
    x_ref, masks, line = place
    columns = wo_ref.shape[2]
    loads = []
    for i, (group, mask) in enumerate(masks):
        block = line * group + jnp.bitwise_xor(x_ref[0], mask)
        columns_of = pl.ds(pl.multiple_of(block * columns, 128), columns)
        loads.append(start(wo_in.at[:, columns_of], wo_ref.at[i], sem.at[i]))
    return loads


def products(rows, loads, wo_ref, a_ref, b_ref):
    for i in range(4):
        loads[i].wait()
        (a_ref, b_ref)[i // 2][i % 2] = nn(rows, wo_ref[i]).astype(BF16)


def first_products_kernel(
    masks, line, x_ref, q_in, wg_ref, wu_ref, wd_ref, wo_in, a_ref, b_ref, rows_ref, q_ref, wo_ref, sem, wo_sem
):
    query = start(q_in, q_ref, sem)
    loads = blocks_of((x_ref, masks, line), wo_in, wo_ref, wo_sem)
    query.wait()
    q = q_ref[...]
    x = nn(q, wg_ref[0])
    act = (jax.nn.silu(x) * nn(q, wu_ref[0])).astype(BF16)
    raw = nn(act, wd_ref[0])
    rows = (raw * lax.rsqrt(jnp.mean(raw * raw, axis=-1, keepdims=True) + 1e-6)).astype(BF16)
    rows_ref[...] = rows
    products(rows, loads, wo_ref, a_ref, b_ref)


def later_products_kernel(masks, line, x_ref, rows_ref, wo_in, a_ref, b_ref, wo_ref, wo_sem):
    loads = blocks_of((x_ref, masks, line), wo_in, wo_ref, wo_sem)
    products(rows_ref[...], loads, wo_ref, a_ref, b_ref)


def first_products(masks, line, x, q, weights, w_out, heads):
    rows, features = q.shape
    columns = w_out.shape[1] // heads
    pair = pltpu.VMEM((2, rows, columns), BF16)
    return pl.pallas_call(
        functools.partial(first_products_kernel, masks, line),
        out_shape=(pair, pair, pltpu.VMEM((rows, features), BF16)),
        in_specs=[SMEM, HBM, VMEM, VMEM, VMEM, HBM],
        out_specs=(VMEM,) * 3,
        scratch_shapes=[
            pltpu.VMEM((rows, features), BF16),
            pltpu.VMEM((4, features, columns), BF16),
            pltpu.SemaphoreType.DMA,
            pltpu.SemaphoreType.DMA((4,)),
        ],
        compiler_params=ROOM,
    )(x, q, *weights, w_out)


def later_products(masks, line, x, rows, w_out, heads):
    features = rows.shape[1]
    columns = w_out.shape[1] // heads
    pair = pltpu.VMEM((2, rows.shape[0], columns), BF16)
    return pl.pallas_call(
        functools.partial(later_products_kernel, masks, line),
        out_shape=(pair, pair),
        in_specs=[SMEM, VMEM, HBM],
        out_specs=(VMEM, VMEM),
        scratch_shapes=[pltpu.VMEM((4, features, columns), BF16), pltpu.SemaphoreType.DMA((4,))],
        compiler_params=ROOM,
    )(x, rows, w_out)


def halve_kernel(a_ref, ar_ref, b_ref, br_ref, a_keep, a_send, b_keep, b_send):
    for kept, come, keep, send in ((a_ref, ar_ref, a_keep, a_send), (b_ref, br_ref, b_keep, b_send)):
        keep[...] = (kept[0].astype(F32) + come[0].astype(F32)).astype(BF16)
        send[...] = (kept[1].astype(F32) + come[1].astype(F32)).astype(BF16)


def halve(a, a_come, b, b_come):
    shape = jax.ShapeDtypeStruct(a.shape[1:], BF16)
    return call(halve_kernel, (shape,) * 4, (a, a_come, b, b_come))


def choose_kernel(far_ref, a_ref, ar_ref, b_ref, br_ref, keep_ref, send_ref):
    a = (a_ref[...].astype(F32) + ar_ref[...].astype(F32)).astype(BF16)
    b = (b_ref[...].astype(F32) + br_ref[...].astype(F32)).astype(BF16)
    second = far_ref[0] == 1
    keep_ref[...] = jnp.where(second, b, a)
    send_ref[...] = jnp.where(second, a, b)


def choose(far, a, a_come, b, b_come):
    shape = jax.ShapeDtypeStruct(a.shape, BF16)
    return call(choose_kernel, (shape, shape), (far, a, a_come, b, b_come), smem=1)


def attend_kernel(position_ref, q_ref, k_ref, v_ref, kp_ref, vp_ref, out_ref):
    rows = q_ref.shape[0]
    has_prior = position_ref[0] > 0
    row = lax.broadcasted_iota(jnp.int32, (rows, rows), 0)
    column = lax.broadcasted_iota(jnp.int32, (rows, rows), 1)
    here = column <= row
    for h in range(q_ref.shape[1] // AD):
        cols = slice(h * AD, (h + 1) * AD)
        q = q_ref[:, cols]
        now = nt(q, k_ref[:, cols])
        before = nt(q, kp_ref[:, cols])
        before = jnp.where(has_prior, before * AD**-0.5, -1e30)
        scores = jnp.where(here, now * AD**-0.5, before)
        e = jnp.exp(scores - jnp.max(scores, axis=-1, keepdims=True))
        probs = e / jnp.sum(e, axis=-1, keepdims=True)
        probs_now = jnp.where(here, probs, 0.0).astype(BF16)
        probs_before = jnp.where(here, 0.0, probs).astype(BF16)
        out_ref[:, cols] = nn(probs_now, v_ref[:, cols]) + nn(probs_before, vp_ref[:, cols])


def attend(position, q, k, v, k_prior, v_prior):
    return call(
        attend_kernel, pltpu.VMEM(q.shape, F32), (position, q, k, v, k_prior, v_prior), smem=1
    )


def swap(x, axis):
    return lax.ppermute(x, axis, [(0, 1), (1, 0)])


def half_sum(own, come):
    return (own.astype(F32) + come.astype(F32)).astype(BF16)


def block_sum(half):
    arrived = lax.all_to_all(half, CHIPS, 0, 0, tiled=True)
    return arrived.astype(F32).sum(axis=0).astype(BF16)


def from_every_chip(share):
    copies = jnp.broadcast_to(share, (lax.axis_size(CHIPS), *share.shape))
    return lax.all_to_all(near(copies), CHIPS, 0, 0, tiled=True)


def near(x):
    return pltpu.with_memory_space_constraint(x, pltpu.VMEM)


def stored(x):
    return pltpu.with_memory_space_constraint(x, pltpu.HBM)


def together(*arrays):
    return lax.optimization_barrier(arrays)


def flip(x, mask):
    devices = range(lax.axis_size(HEAD[1]))
    return lax.ppermute(x, HEAD[1], [(i, i ^ mask) for i in devices])


def on_device(fast_q, fast_k, fast_v, rates, w_gate, w_up, w_down, w_out, att_q, att_k, att_v):
    chips = lax.axis_size(CHIPS)
    heads = lax.axis_size(HEAD)
    core = lax.axis_index("core").astype(jnp.int32).reshape(1)
    seat = lax.axis_index(SEQ[1:]).astype(jnp.int32).reshape(1)
    span = lax.axis_index("span")
    position = lax.axis_index(SEQ).astype(jnp.int32).reshape(1)
    seats = lax.axis_size(SEQ)
    far = lax.axis_index(HEAD[0]).astype(jnp.int32).reshape(1)
    x = lax.axis_index(HEAD[1]).astype(jnp.int32).reshape(1)
    line = lax.axis_size(HEAD[1])
    fast_q, fast_k, fast_v, rates, w_out = map(stored, (fast_q, fast_k, fast_v, rates, w_out))
    weights = tuple(map(stored, (w_gate, w_up, w_down)))

    route = [(i, i + 1) for i in range(seats - 1)]
    k_prior = lax.ppermute(att_k, SEQ, route)
    v_prior = lax.ppermute(att_v, SEQ, route)

    own, away = gradients(core, fast_k, fast_v, rates, weights, chips)
    share = block_sum(half_sum(own, swap(away, "core")))
    given = lax.ppermute(share, "span", [(0, 1)])
    k_prior, v_prior, share = together(k_prior, v_prior, share)
    attended = attend(position, att_q, att_k, att_v, near(k_prior), near(v_prior))
    given, attended = together(given, attended)
    own = from_every_chip(given)
    weights, own, away = update(core, rates, near(own), near(swap(own, "core")), weights, fast_k, fast_v)

    sent = ((0, 1), (0, 2), (1, 3), (1, 2))
    held = ((0, 0), (0, 3), (1, 0), (1, 1))
    come = swap(away, "core")
    a_sent, b_sent, rows = first_products(sent, line, x, fast_q, weights, w_out, heads)
    come, a_sent, b_sent, rows = together(come, a_sent, b_sent, rows)
    a_come = flip(a_sent, 1)
    b_come = flip(b_sent, 3)
    a_held, b_held = later_products(held, line, x, rows, w_out, heads)
    share = block_sum(half_sum(own, come))
    a_held, a_sent, b_held, b_sent = halve(a_held, near(a_come), b_held, near(b_come))
    a_come = flip(a_sent, 3)
    b_come = flip(b_sent, 1)
    own = from_every_chip(share)
    held, sent = choose(far, a_held, near(a_come), b_held, near(b_come))
    come = swap(sent, HEAD[0])
    away = swap(own, "core")

    mine, peer = last_update(core, seat, near(own), near(away), weights, w_gate.shape[1] // seats)
    given = lax.ppermute(peer, "span", [(1, 0)])
    final = jnp.where(span == 1, mine, given)[:, None]
    mixed = (attended + held.astype(F32) + come.astype(F32)).astype(BF16)
    return mixed, final


def solution(mesh):
    split = Mesh(mesh.devices.reshape(2, 2, 4, 2, 2, 4), (*SEQ, *HEAD))
    in_specs = (
        P(SEQ, HEAD),
        P(SEQ, HEAD),
        P(SEQ, HEAD),
        P(HEAD, SEQ),
        P(HEAD, None, None),
        P(HEAD, None, None),
        P(HEAD, None, None),
        P(HEAD, None),
        P(SEQ, HEAD),
        P(SEQ, HEAD),
        P(SEQ, HEAD),
    )
    out_specs = (P(SEQ, HEAD), P(None, HEAD, SEQ, None))
    return jax.shard_map(on_device, mesh=split, in_specs=in_specs, out_specs=out_specs, check_vma=False)
```

time: 165 us -> 156 us (0.945)
  blocking collectives: 21.6 us -> 37.7 us
  waiting for transfers between devices: 49.9 us -> 34.3 us
  Pallas kernels: 44.2 us -> 35.5 us
  local copies, waits for them, and re-layouts: 1.08 us -> 6.17 us
  starting transfers between devices: 38.9 us -> 33.9 us
    all_to_all x1 -> x2, blocking collectives: 21.6 us -> 37.7 us  [the longest x1 21.6 us: from_every_chip(): return lax.all_to_all(near(copies), CHIPS, 0, 0, tiled=True)]
    ppermute x4, waiting for transfers between devices: 24.9 us -> 12 us  [flip(): return lax.ppermute(x, HEAD[1], [(i, i ^ mask) for i in devices])]
    all_to_all x1, waiting for transfers between devices: 0.01 us -> 6.96 us  [from_every_chip(): return lax.all_to_all(near(copies), CHIPS, 0, 0, tiled=True)]
    all_to_all x2 -> x1, waiting for transfers between devices: 12.2 us -> 5.71 us  [block_sum(): arrived = lax.all_to_all(half, CHIPS, 0, 0, tiled=True)]
    ppermute x5, waiting for transfers between devices: 10.9 us -> 4.56 us  [swap(): return lax.ppermute(x, axis, [(0, 1), (1, 0)])]
    all_to_all x2 -> x1, starting transfers between devices: 11.5 us -> 6.4 us  [block_sum(): arrived = lax.all_to_all(half, CHIPS, 0, 0, tiled=True)]
    unnamed x16 -> x22, local copies, waits for them, and re-layouts: 0.03 us -> 5.11 us
    pallas_call x3, Pallas kernels: 21.9 us -> 17.1 us  [the longest x1 10.6 us: update(): pl.pallas_call(update_kernel, compiler_params=ROOM, out_shape=(weight,) *...]
  transfers between devices with their start and end apart: 16 -> 15, of which waited for: 10 -> 8; matrix products, arithmetic and copies ran while one was open for 1% -> 1% of each run, Pallas kernels for 17% -> 14%
where the time goes in v1:
time: 156 us; the launch traced here: 154 us
  blocking collectives  37.7 us (24%)
  Pallas kernels  35.5 us (23%)
  waiting for transfers between devices  34.3 us (22%)
  starting transfers between devices  33.9 us (22%)
  local copies, waits for them, and re-layouts  6.17 us (4%)
  other arithmetic  5.68 us (4%)
    all_to_all x1, blocking collectives, from_every_chip(): return lax.all_to_all(near(copies), CHIPS, 0, 0, tiled=True)  21.6 us
    all_to_all x1, blocking collectives, block_sum(): arrived = lax.all_to_all(half, CHIPS, 0, 0, tiled=True)  16 us
    ppermute x4, waiting for transfers between devices, flip(): return lax.ppermute(x, HEAD[1], [(i, i ^ mask) for i in devices])  12 us
    pallas_call x1, Pallas kernels, update(): pl.pallas_call(update_kernel, compiler_params=ROOM, out_shape=(weight,) *...  10.6 us
    pallas_call x1, Pallas kernels, last_update(): pl.pallas_call(last_kernel, out_shape=(shape, shape), in_specs=[SMEM, SME...  8.09 us
    all_to_all x1, waiting for transfers between devices, from_every_chip(): return lax.all_to_all(near(copies), CHIPS, 0, 0, tiled=True)  6.96 us
    all_to_all x1, starting transfers between devices, block_sum(): arrived = lax.all_to_all(half, CHIPS, 0, 0, tiled=True)  6.4 us
    pallas_call x3, Pallas kernels, call(): pl.pallas_call(kernel, out_shape=outs, in_specs=[SMEM] * smem + [VMEM] *...  6.27 us
  transfers between devices with their start and end apart: 15, of which 8 were waited for; matrix products, arithmetic and copies ran while one was open for 1% of the time, Pallas kernels for 14%

profile of v1, /device:TPU:8, one launch (start us, length us, event | category | flops | bytes accessed | tf_op | source)
XLA Modules:
  0.0 154.1 jit_solution(17810107139021684546)
XLA Ops:
  0.6 4.0 %shard_map.122 = (bf16[8,3,32,512]{3,2,1,0:T(8,128)(2,1)S(1)}, bf16[8,3,32,512]{3,2,1,0:T(8,128)(2,1)S(1)}) custom-call(s32[1]{0:T(128)} %bitcast.core_ref, f32[1,256]{1,0:T(1,128)} %rate_in.3, bf16[256,512]{1,0:T(8,128)(2,1)} %k_in.3, bf16[256,512]{1,0:T(8,128)(2,1)} %v_in.3, bf16[1,512,512]{2,1,0:T(8,128)(2,1)} %wg_in.3, bf16[1,512,512]{2,1,0:T(8,128)(2,1)} %wu_in.3, ...), custom_call_target="tpu_custom_call" | custom-call | tf_op jit(solution)/shard_map/pallas_call | solution.py:122
  4.7 0.1 collective-permute-start
  4.8 2.3 %collective-permute-done = bf16[8,3,32,512]{3,2,1,0:T(8,128)(2,1)S(1)} collective-permute-done((bf16[8,3,32,512]{3,2,1,0:T(8,128)(2,1)S(1)}, bf16[8,3,32,512]{3,2,1,0:T(8,128)(2,1)S(1)}, u32[]{:S(2)}, u32[]{:S(2)}) %collective-permute-start) | collective-permute-done | bytes 786464 | tf_op jit(solution)/shard_map/ppermute | solution.py:372
  7.0 0.0 copy-start.1
  7.1 1.2 add_convert_fusion.1
  8.2 0.0 copy-start
  8.2 6.4 %all-to-all-start = ((bf16[8,3,32,512]{3,2,1,0:T(8,128)(2,1)}), bf16[8,3,32,512]{3,2,1,0:T(8,128)(2,1)S(1)}, u32[]{:S(2)}, u32[]{:S(2)}) async-start(bf16[8,3,32,512]{3,2,1,0:T(8,128)(2,1)} %add_convert_fusion.1), calls=%async_computation | async-start | bytes 1572864 | tf_op jit(solution)/shard_map/all_to_all | solution.py:380
  14.6 0.0 copy-done.1
  14.6 1.9 %collective-permute-start.2 = (bf16[256,640]{1,0:T(8,128)(2,1)S(1)}, bf16[256,640]{1,0:T(8,128)(2,1)S(1)}, u32[]{:S(2)}, u32[]{:S(2)}) collective-permute-start(bf16[256,640]{1,0:T(8,128)(2,1)S(1)} %copy-done.1), channel_id=1, source_target_pairs={{0,8},{8,16},{16,24},{24,32},{32,40},{40,48},{48,56},{56,64},{64,7... | collective-permute-start | bytes 983048 | tf_op jit(solution)/shard_map/ppermute | solution.py:421
  16.5 0.0 copy-done.2
  16.6 3.5 %collective-permute-start.3 = (bf16[256,640]{1,0:T(8,128)(2,1)S(1)}, bf16[256,640]{1,0:T(8,128)(2,1)S(1)}, u32[]{:S(2)}, u32[]{:S(2)}) collective-permute-start(bf16[256,640]{1,0:T(8,128)(2,1)S(1)} %copy-done.2), channel_id=1, source_target_pairs={{0,8},{8,16},{16,24},{24,32},{32,40},{40,48},{48,56},{56,64},{64,7... | collective-permute-start | bytes 983048 | tf_op jit(solution)/shard_map/ppermute | solution.py:422
  20.0 5.7 %all-to-all-done = bf16[8,3,32,512]{3,2,1,0:T(8,128)(2,1)S(1)} async-done(((bf16[8,3,32,512]{3,2,1,0:T(8,128)(2,1)}), bf16[8,3,32,512]{3,2,1,0:T(8,128)(2,1)S(1)}, u32[]{:S(2)}, u32[]{:S(2)}) %all-to-all-start) | async-done | bytes 786464 | tf_op jit(solution)/shard_map/all_to_all | solution.py:380
  25.8 0.1 reduce_sum.24
  25.9 5.2 %collective-permute-start.1 = (bf16[3,32,512]{2,1,0:T(8,128)(2,1)S(1)}, bf16[3,32,512]{2,1,0:T(8,128)(2,1)S(1)}, u32[]{:S(2)}, u32[]{:S(2)}) collective-permute-start(bf16[3,32,512]{2,1,0:T(8,128)(2,1)S(1)} %reduce_sum.24), channel_id=1, source_target_pairs={{0,128},{1,129},{2,130},{3,131},{4,132},{5,133},{6,134},{7,135},{8... | collective-permute-start | bytes 294920 | tf_op jit(solution)/shard_map/ppermute | solution.py:426
  31.1 0.0 collective-permute-done.2.kp_ref
  31.1 0.0 collective-permute-done.3.vp_ref
  31.1 0.0 copy-done
  31.1 2.2 %shard_map.123 = f32[256,640]{1,0:T(8,128)S(1)} custom-call(s32[1]{0:T(128)} %bitcast.1.position_ref, bf16[256,640]{1,0:T(8,128)(2,1)S(1)} %copy-done, bf16[256,640]{1,0:T(8,128)(2,1)S(1)} %copy-done.1, bf16[256,640]{1,0:T(8,128)(2,1)S(1)} %copy-done.2, bf16[256,640]{1,0:T(8,128)(2,1)S(1)} %collective-permute-done.2.kp_ref, ...), custom_call_target="tpu_custom_call" | custom-call | tf_op jit(solution)/shard_map/pallas_call | solution.py:40
  33.3 0.0 collective-permute-done.1
  33.3 0.1 broadcast_in_dim.9
  33.4 21.6 %all_to_all.20.own_in = bf16[8,3,32,512]{3,2,1,0:T(8,128)(2,1)S(1)} all-to-all(bf16[8,3,32,512]{3,2,1,0:T(8,128)(2,1)S(1)} %broadcast_in_dim.9), channel_id=1, replica_groups=mesh['span'=2,'row'=2,'y'=4,'core'=2,'head_0'=2,'head_1'=4] {'row','y'}, dimensions={0} | all-to-all | bytes 1572864 | tf_op jit(solution)/shard_map/all_to_all | solution.py:386
  55.0 0.0 collective-permute-start.4
  55.0 2.3 %collective-permute-done.4.far_in = bf16[8,3,32,512]{3,2,1,0:T(8,128)(2,1)S(1)} collective-permute-done((bf16[8,3,32,512]{3,2,1,0:T(8,128)(2,1)S(1)}, bf16[8,3,32,512]{3,2,1,0:T(8,128)(2,1)S(1)}, u32[]{:S(2)}, u32[]{:S(2)}) %collective-permute-start.4) | collective-permute-done | bytes 786464 | tf_op jit(solution)/shard_map/ppermute | solution.py:372
  57.3 10.6 %shard_map.124 = (bf16[1,512,512]{2,1,0:T(8,128)(2,1)S(1)}, bf16[1,512,512]{2,1,0:T(8,128)(2,1)S(1)}, bf16[1,512,512]{2,1,0:T(8,128)(2,1)S(1)}, bf16[8,3,32,512]...) custom-call(s32[1]{0:T(128)} %bitcast.core_ref, f32[1,256]{1,0:T(1,128)} %rate_in.3, ...), custom_call_target="tpu_custom_call" | custom-call | tf_op jit(solution)/shard_map/pallas_call | solution.py:202
  67.9 0.2 collective-permute-start.5
  68.2 3.8 %shard_map.125 = (bf16[2,256,640]{2,1,0:T(8,128)(2,1)S(1)}, bf16[2,256,640]{2,1,0:T(8,128)(2,1)S(1)}, bf16[256,512]{1,0:T(8,128)(2,1)S(1)}) custom-call(s32[1]{0:T(128)} %bitcast.3.x_ref, bf16[256,512]{1,0:T(8,128)(2,1)} %q_in.1, bf16[1,512,512]{2,1,0:T(8,128)(2,1)S(1)} %get-tuple-element.37.wg_ref, bf16[1,512,512]{2,1,0:T(8,128)(2,1)S(1)} %get-tuple-element.38.wu_ref, ...), custom_call_target="tpu_custom_call" | custom-call | tf_op jit(solution)/shard_map/pallas_call | solution.py:292
  72.0 0.0 copy-start.9
  72.0 0.0 copy-start.10
  72.0 0.0 collective-permute-done.5
  72.0 1.9 %add_convert_fusion = bf16[8,3,32,512]{3,2,1,0:T(8,128)(2,1)S(1)} fusion(bf16[8,3,32,512]{3,2,1,0:T(8,128)(2,1)} %collective-permute-done.5, bf16[8,3,32,512]{3,2,1,0:T(8,128)(2,1)S(1)} %get-tuple-element.54), kind=kLoop, calls=%fused_computation | loop fusion | flops 1572864 | bytes 2359296 | tf_op jit(solution)/shard_map/convert_element_type | solution.py:376
  73.9 0.0 copy-done.9
  73.9 0.0 copy-done.10
  73.9 16.0 %all_to_all.21 = bf16[8,3,32,512]{3,2,1,0:T(8,128)(2,1)S(1)} all-to-all(bf16[8,3,32,512]{3,2,1,0:T(8,128)(2,1)S(1)} %add_convert_fusion), channel_id=1, replica_groups=mesh['span'=2,'row'=2,'y'=4,'core'=2,'head_0'=2,'head_1'=4] {'row','y'}, dimensions={0} | all-to-all | bytes 1572864 | tf_op jit(solution)/shard_map/all_to_all | solution.py:380
  89.9 0.1 reduce_sum.25
  90.1 1.0 broadcast_in_dim.10
  91.0 5.1 %all-to-all-start.3 = ((bf16[8,3,32,512]{3,2,1,0:T(8,128)(2,1)}), bf16[8,3,32,512]{3,2,1,0:T(8,128)(2,1)S(1)}, u32[]{:S(2)}, u32[]{:S(2)}) async-start(bf16[8,3,32,512]{3,2,1,0:T(8,128)(2,1)} %broadcast_in_dim.10), calls=%async_computation.3 | async-start | bytes 1572864 | tf_op jit(solution)/shard_map/all_to_all | solution.py:386
  96.2 1.5 collective-permute-start.6
  97.7 2.1 %collective-permute-start.7 = (bf16[2,256,640]{2,1,0:T(8,128)(2,1)}, bf16[2,256,640]{2,1,0:T(8,128)(2,1)}, u32[]{:S(2)}, u32[]{:S(2)}) collective-permute-start(bf16[2,256,640]{2,1,0:T(8,128)(2,1)} %copy-done.9), channel_id=1, source_target_pairs={{0,3},{1,2},{2,1},{3,0},{4,7},{5,6},{6,5},{7,4},{8,11},{9,10},{10,... | collective-permute-start | bytes 1966088 | tf_op jit(solution)/shard_map/ppermute | solution.py:403
  99.8 7.0 %all-to-all-done.3.own_in = bf16[8,3,32,512]{3,2,1,0:T(8,128)(2,1)S(1)} async-done(((bf16[8,3,32,512]{3,2,1,0:T(8,128)(2,1)}), bf16[8,3,32,512]{3,2,1,0:T(8,128)(2,1)S(1)}, u32[]{:S(2)}, u32[]{:S(2)}) %all-to-all-start.3) | async-done | bytes 786464 | tf_op jit(solution)/shard_map/all_to_all | solution.py:386
  106.7 0.0 collective-permute-start.11
  106.7 2.6 %shard_map.126 = (bf16[2,256,640]{2,1,0:T(8,128)(2,1)S(1)}, bf16[2,256,640]{2,1,0:T(8,128)(2,1)S(1)}) custom-call(s32[1]{0:T(128)} %bitcast.3.x_ref, bf16[256,512]{1,0:T(8,128)(2,1)S(1)} %get-tuple-element.43.rows_ref, bf16[512,5120]{1,0:T(8,128)(2,1)} %wo_in.3), custom_call_target="tpu_custom_call" | custom-call | tf_op jit(solution)/shard_map/pallas_call | solution.py:311
  109.3 2.8 %collective-permute-done.6.ar_ref = bf16[2,256,640]{2,1,0:T(8,128)(2,1)} collective-permute-done((bf16[2,256,640]{2,1,0:T(8,128)(2,1)}, bf16[2,256,640]{2,1,0:T(8,128)(2,1)}, u32[]{:S(2)}, u32[]{:S(2)}) %collective-permute-start.6) | collective-permute-done | bytes 655392 | tf_op jit(solution)/shard_map/ppermute | solution.py:403
  112.1 2.4 %collective-permute-done.7.br_ref = bf16[2,256,640]{2,1,0:T(8,128)(2,1)} collective-permute-done((bf16[2,256,640]{2,1,0:T(8,128)(2,1)}, bf16[2,256,640]{2,1,0:T(8,128)(2,1)}, u32[]{:S(2)}, u32[]{:S(2)}) %collective-permute-start.7) | collective-permute-done | bytes 655392 | tf_op jit(solution)/shard_map/ppermute | solution.py:403
  114.5 2.2 %shard_map.127 = (bf16[256,640]{1,0:T(8,128)(2,1)S(1)}, bf16[256,640]{1,0:T(8,128)(2,1)}, bf16[256,640]{1,0:T(8,128)(2,1)S(1)}, bf16[256,640]{1,0:T(8,128)(2,1)}) custom-call(bf16[2,256,640]{2,1,0:T(8,128)(2,1)S(1)} %get-tuple-element.44.a_ref, bf16[2,256,640]{2,1,0:T(8,128)(2,1)} %collective-permute-done.6.ar_ref, ...), custom_call_target="tpu_custom_call" | custom-call | tf_op jit(solution)/shard_map/pallas_call | solution.py:40
  116.8 0.0 copy-start.3
  116.8 0.7 copy-done.3
  117.5 0.7 copy-done.5
  118.2 2.1 %collective-permute-start.8 = (bf16[256,640]{1,0:T(8,128)(2,1)}, bf16[256,640]{1,0:T(8,128)(2,1)S(1)}, u32[]{:S(2)}, u32[]{:S(2)}) collective-permute-start(bf16[256,640]{1,0:T(8,128)(2,1)} %get-tuple-element.49), channel_id=1, source_target_pairs={{0,3},{1,2},{2,1},{3,0},{4,7},{5,6},{6,5},{7,4},{8,11},{9,10},{10,... | collective-permute-start | bytes 983048 | tf_op jit(solution)/shard_map/ppermute | solution.py:403
  120.3 0.0 collective-permute-start.9
  120.3 6.8 %collective-permute-done.8.ar_ref = bf16[256,640]{1,0:T(8,128)(2,1)S(1)} collective-permute-done((bf16[256,640]{1,0:T(8,128)(2,1)}, bf16[256,640]{1,0:T(8,128)(2,1)S(1)}, u32[]{:S(2)}, u32[]{:S(2)}) %collective-permute-start.8) | collective-permute-done | bytes 327712 | tf_op jit(solution)/shard_map/ppermute | solution.py:403
  127.1 0.7 copy-done.7
  127.8 0.0 collective-permute-done.9.br_ref
  127.8 1.0 copy-done.4
  128.8 1.0 copy-done.6
  129.8 1.0 copy-done.8
  130.7 1.9 %shard_map.128 = (bf16[256,640]{1,0:T(8,128)(2,1)S(1)}, bf16[256,640]{1,0:T(8,128)(2,1)}) custom-call(s32[1]{0:T(128)} %bitcast.2.far_ref, bf16[256,640]{1,0:T(8,128)(2,1)S(1)} %copy-done.4, bf16[256,640]{1,0:T(8,128)(2,1)S(1)} %copy-done.8, bf16[256,640]{1,0:T(8,128)(2,1)S(1)} %copy-done.6, bf16[256,640]{1,0:T(8,128)(2,1)} %collective-permute-done.9.br_ref), custom_call_target="tpu_custom_call" | custom-call | tf_op jit(solution)/shard_map/pallas_call | solution.py:40
  132.6 4.5 %collective-permute-start.10 = (bf16[256,640]{1,0:T(8,128)(2,1)}, bf16[256,640]{1,0:T(8,128)(2,1)}, u32[]{:S(2)}, u32[]{:S(2)}) collective-permute-start(bf16[256,640]{1,0:T(8,128)(2,1)} %get-tuple-element.53), channel_id=1, source_target_pairs={{0,4},{4,0},{1,5},{5,1},{2,6},{6,2},{3,7},{7,3},{8,12},{12,8},{9,1... | collective-permute-start | bytes 983048 | tf_op jit(solution)/shard_map/ppermute | solution.py:372
  137.1 0.0 collective-permute-done.11.far_in
  137.1 8.1 %shard_map.129 = (bf16[3,16,512]{2,1,0:T(8,128)(2,1)S(1)}, bf16[3,16,512]{2,1,0:T(8,128)(2,1)S(1)}) custom-call(s32[1]{0:T(128)} %bitcast.core_ref, s32[1]{0:T(128)} %bitcast.4.seat_ref, bf16[8,3,32,512]{3,2,1,0:T(8,128)(2,1)S(1)} %all-to-all-done.3.own_in, bf16[8,3,32,512]{3,2,1,0:T(8,128)(2,1)} %collective-permute-done.11.far_in, ...), custom_call_target="tpu_custom_call" | custom-call | tf_op jit(solution)/shard_map/pallas_call | solution.py:237
  145.2 1.3 collective-permute-start.12
  146.5 0.0 collective-permute-done.10
  146.5 1.8 %add_convert_fusion.2 = bf16[256,640]{1,0:T(8,128)(2,1)} fusion(bf16[256,640]{1,0:T(8,128)(2,1)} %collective-permute-done.10, f32[256,640]{1,0:T(8,128)S(1)} %shard_map.123, bf16[256,640]{1,0:T(8,128)(2,1)S(1)} %get-tuple-element.52), kind=kLoop, calls=%fused_computation.2 | loop fusion | flops 819200 | bytes 1638400 | tf_op jit(solution)/shard_map/convert_element_type | solution.py:453
  148.3 5.1 %collective-permute-done.12 = bf16[3,16,512]{2,1,0:T(8,128)(2,1)S(1)} collective-permute-done((bf16[3,16,512]{2,1,0:T(8,128)(2,1)S(1)}, bf16[3,16,512]{2,1,0:T(8,128)(2,1)S(1)}, u32[]{:S(2)}, u32[]{:S(2)}) %collective-permute-start.12) | collective-permute-done | bytes 49184 | tf_op jit(solution)/shard_map/ppermute | solution.py:451
  153.4 0.6 select_bitcast_fusion
  (6 shorter events, 0.0 us)
Async XLA Ops:
  4.7 2.4 %collective-permute-start = (bf16[8,3,32,512]{3,2,1,0:T(8,128)(2,1)S(1)}, bf16[8,3,32,512]{3,2,1,0:T(8,128)(2,1)S(1)}, u32[]{:S(2)}, u32[]{:S(2)}) collective-permute-start(bf16[8,3,32,512]{3,2,1,0:T(8,128)(2,1)S(1)} %get-tuple-element.31), channel_id=1, source_target_pairs={{0,8},{8,0},{1,9},{9,1},{2,10},{10,2},{3,11},{11,3},{4,12},{12,4},... | collective-permute-start | bytes 2359304 | tf_op jit(solution)/shard_map/ppermute | solution.py:372
  7.0 7.6 %copy-start.1 = (bf16[256,640]{1,0:T(8,128)(2,1)S(1)}, bf16[256,640]{1,0:T(8,128)(2,1)}, u32[]{:S(2)}) copy-start(bf16[256,640]{1,0:T(8,128)(2,1)} %k_ref.1) | copy-start | bytes 983044
  7.1 9.5 %copy-start.2 = (bf16[256,640]{1,0:T(8,128)(2,1)S(1)}, bf16[256,640]{1,0:T(8,128)(2,1)}, u32[]{:S(2)}) copy-start(bf16[256,640]{1,0:T(8,128)(2,1)} %v_ref.1) | copy-start | bytes 983044
  8.2 22.9 %copy-start = (bf16[256,640]{1,0:T(8,128)(2,1)S(1)}, bf16[256,640]{1,0:T(8,128)(2,1)}, u32[]{:S(2)}) copy-start(bf16[256,640]{1,0:T(8,128)(2,1)} %q_ref.1) | copy-start | bytes 983044
  8.2 17.5 %all-to-all-start = ((bf16[8,3,32,512]{3,2,1,0:T(8,128)(2,1)}), bf16[8,3,32,512]{3,2,1,0:T(8,128)(2,1)S(1)}, u32[]{:S(2)}, u32[]{:S(2)}) async-start(bf16[8,3,32,512]{3,2,1,0:T(8,128)(2,1)} %add_convert_fusion.1), calls=%async_computation | async-start | bytes 1572864 | tf_op jit(solution)/shard_map/all_to_all | solution.py:380
  14.6 16.4 %collective-permute-start.2 = (bf16[256,640]{1,0:T(8,128)(2,1)S(1)}, bf16[256,640]{1,0:T(8,128)(2,1)S(1)}, u32[]{:S(2)}, u32[]{:S(2)}) collective-permute-start(bf16[256,640]{1,0:T(8,128)(2,1)S(1)} %copy-done.1), channel_id=1, source_target_pairs={{0,8},{8,16},{16,24},{24,32},{32,40},{40,48},{48,56},{56,64},{64,7... | collective-permute-start | bytes 983048 | tf_op jit(solution)/shard_map/ppermute | solution.py:421
  16.6 14.5 %collective-permute-start.3 = (bf16[256,640]{1,0:T(8,128)(2,1)S(1)}, bf16[256,640]{1,0:T(8,128)(2,1)S(1)}, u32[]{:S(2)}, u32[]{:S(2)}) collective-permute-start(bf16[256,640]{1,0:T(8,128)(2,1)S(1)} %copy-done.2), channel_id=1, source_target_pairs={{0,8},{8,16},{16,24},{24,32},{32,40},{40,48},{48,56},{56,64},{64,7... | collective-permute-start | bytes 983048 | tf_op jit(solution)/shard_map/ppermute | solution.py:422
  25.9 7.4 %collective-permute-start.1 = (bf16[3,32,512]{2,1,0:T(8,128)(2,1)S(1)}, bf16[3,32,512]{2,1,0:T(8,128)(2,1)S(1)}, u32[]{:S(2)}, u32[]{:S(2)}) collective-permute-start(bf16[3,32,512]{2,1,0:T(8,128)(2,1)S(1)} %reduce_sum.24), channel_id=1, source_target_pairs={{0,128},{1,129},{2,130},{3,131},{4,132},{5,133},{6,134},{7,135},{8... | collective-permute-start | bytes 294920 | tf_op jit(solution)/shard_map/ppermute | solution.py:426
  55.0 2.3 %collective-permute-start.4 = (bf16[8,3,32,512]{3,2,1,0:T(8,128)(2,1)S(1)}, bf16[8,3,32,512]{3,2,1,0:T(8,128)(2,1)S(1)}, u32[]{:S(2)}, u32[]{:S(2)}) collective-permute-start(bf16[8,3,32,512]{3,2,1,0:T(8,128)(2,1)S(1)} %all_to_all.20.own_in), channel_id=1, source_target_pairs={{0,8},{8,0},{1,9},{9,1},{2,10},{10,2},{3,11},{11,3},{4,12},{12,4},... | collective-permute-start | bytes 2359304 | tf_op jit(solution)/shard_map/ppermute | solution.py:372
  67.9 4.1 %collective-permute-start.5 = (bf16[8,3,32,512]{3,2,1,0:T(8,128)(2,1)}, bf16[8,3,32,512]{3,2,1,0:T(8,128)(2,1)}, u32[]{:S(2)}, u32[]{:S(2)}) collective-permute-start(bf16[8,3,32,512]{3,2,1,0:T(8,128)(2,1)} %get-tuple-element.36), channel_id=1, source_target_pairs={{0,8},{8,0},{1,9},{9,1},{2,10},{10,2},{3,11},{11,3},{4,12},{12,4},... | collective-permute-start | bytes 2359304 | tf_op jit(solution)/shard_map/ppermute | solution.py:372
  72.0 1.9 %copy-start.9 = (bf16[2,256,640]{2,1,0:T(8,128)(2,1)}, bf16[2,256,640]{2,1,0:T(8,128)(2,1)S(1)}, u32[]{:S(2)}) copy-start(bf16[2,256,640]{2,1,0:T(8,128)(2,1)S(1)} %get-tuple-element.47) | copy-start | bytes 1966084
  72.0 1.9 %copy-start.10 = (bf16[2,256,640]{2,1,0:T(8,128)(2,1)}, bf16[2,256,640]{2,1,0:T(8,128)(2,1)S(1)}, u32[]{:S(2)}) copy-start(bf16[2,256,640]{2,1,0:T(8,128)(2,1)S(1)} %get-tuple-element.45) | copy-start | bytes 1966084
  91.0 15.7 %all-to-all-start.3 = ((bf16[8,3,32,512]{3,2,1,0:T(8,128)(2,1)}), bf16[8,3,32,512]{3,2,1,0:T(8,128)(2,1)S(1)}, u32[]{:S(2)}, u32[]{:S(2)}) async-start(bf16[8,3,32,512]{3,2,1,0:T(8,128)(2,1)} %broadcast_in_dim.10), calls=%async_computation.3 | async-start | bytes 1572864 | tf_op jit(solution)/shard_map/all_to_all | solution.py:386
  96.2 16.0 %collective-permute-start.6 = (bf16[2,256,640]{2,1,0:T(8,128)(2,1)}, bf16[2,256,640]{2,1,0:T(8,128)(2,1)}, u32[]{:S(2)}, u32[]{:S(2)}) collective-permute-start(bf16[2,256,640]{2,1,0:T(8,128)(2,1)} %copy-done.10), channel_id=1, source_target_pairs={{0,1},{1,0},{2,3},{3,2},{4,5},{5,4},{6,7},{7,6},{8,9},{9,8},{10,11... | collective-permute-start | bytes 1966088 | tf_op jit(solution)/shard_map/ppermute | solution.py:403
  97.7 16.9 %collective-permute-start.7 = (bf16[2,256,640]{2,1,0:T(8,128)(2,1)}, bf16[2,256,640]{2,1,0:T(8,128)(2,1)}, u32[]{:S(2)}, u32[]{:S(2)}) collective-permute-start(bf16[2,256,640]{2,1,0:T(8,128)(2,1)} %copy-done.9), channel_id=1, source_target_pairs={{0,3},{1,2},{2,1},{3,0},{4,7},{5,6},{6,5},{7,4},{8,11},{9,10},{10,... | collective-permute-start | bytes 1966088 | tf_op jit(solution)/shard_map/ppermute | solution.py:403
  106.7 30.4 %collective-permute-start.11 = (bf16[8,3,32,512]{3,2,1,0:T(8,128)(2,1)S(1)}, bf16[8,3,32,512]{3,2,1,0:T(8,128)(2,1)}, u32[]{:S(2)}, u32[]{:S(2)}) collective-permute-start(bf16[8,3,32,512]{3,2,1,0:T(8,128)(2,1)S(1)} %all-to-all-done.3.own_in), channel_id=1, source_target_pairs={{0,8},{8,0},{1,9},{9,1},{2,10},{10,2},{3,11},{11,3},{4,12},{12,4},... | collective-permute-start | bytes 2359304 | tf_op jit(solution)/shard_map/ppermute | solution.py:372
  116.8 0.7 copy-start.3
  117.5 0.7 copy-start.5
  118.2 8.9 %collective-permute-start.8 = (bf16[256,640]{1,0:T(8,128)(2,1)}, bf16[256,640]{1,0:T(8,128)(2,1)S(1)}, u32[]{:S(2)}, u32[]{:S(2)}) collective-permute-start(bf16[256,640]{1,0:T(8,128)(2,1)} %get-tuple-element.49), channel_id=1, source_target_pairs={{0,3},{1,2},{2,1},{3,0},{4,7},{5,6},{6,5},{7,4},{8,11},{9,10},{10,... | collective-permute-start | bytes 983048 | tf_op jit(solution)/shard_map/ppermute | solution.py:403
  120.3 7.5 %collective-permute-start.9 = (bf16[256,640]{1,0:T(8,128)(2,1)}, bf16[256,640]{1,0:T(8,128)(2,1)}, u32[]{:S(2)}, u32[]{:S(2)}) collective-permute-start(bf16[256,640]{1,0:T(8,128)(2,1)} %get-tuple-element.51), channel_id=1, source_target_pairs={{0,1},{1,0},{2,3},{3,2},{4,5},{5,4},{6,7},{7,6},{8,9},{9,8},{10,11... | collective-permute-start | bytes 983048 | tf_op jit(solution)/shard_map/ppermute | solution.py:403
  127.1 0.7 copy-start.7
  127.8 1.0 copy-start.4
  128.8 1.0 copy-start.6
  129.8 1.0 copy-start.8
  132.6 13.9 %collective-permute-start.10 = (bf16[256,640]{1,0:T(8,128)(2,1)}, bf16[256,640]{1,0:T(8,128)(2,1)}, u32[]{:S(2)}, u32[]{:S(2)}) collective-permute-start(bf16[256,640]{1,0:T(8,128)(2,1)} %get-tuple-element.53), channel_id=1, source_target_pairs={{0,4},{4,0},{1,5},{5,1},{2,6},{6,2},{3,7},{7,3},{8,12},{12,8},{9,1... | collective-permute-start | bytes 983048 | tf_op jit(solution)/shard_map/ppermute | solution.py:372
  145.2 8.2 %collective-permute-start.12 = (bf16[3,16,512]{2,1,0:T(8,128)(2,1)S(1)}, bf16[3,16,512]{2,1,0:T(8,128)(2,1)S(1)}, u32[]{:S(2)}, u32[]{:S(2)}) collective-permute-start(bf16[3,16,512]{2,1,0:T(8,128)(2,1)S(1)} %get-tuple-element.57), channel_id=1, source_target_pairs={{128,0},{129,1},{130,2},{131,3},{132,4},{133,5},{134,6},{135,7},{1... | collective-permute-start | bytes 147464 | tf_op jit(solution)/shard_map/ppermute | solution.py:451

commit v2 on v1

--- a/solution.py
+++ b/solution.py
@@ -325,8 +325,7 @@
 
 
 def halve(a, a_come, b, b_come):
-    shape = jax.ShapeDtypeStruct(a.shape[1:], BF16)
-    return call(halve_kernel, (shape,) * 4, (a, a_come, b, b_come))
+    return call(halve_kernel, (pltpu.HBM(a.shape[1:], BF16),) * 4, (a, a_come, b, b_come))
 
 
 def choose_kernel(far_ref, a_ref, ar_ref, b_ref, br_ref, keep_ref, send_ref):
@@ -338,8 +337,7 @@
 
 
 def choose(far, a, a_come, b, b_come):
-    shape = jax.ShapeDtypeStruct(a.shape, BF16)
-    return call(choose_kernel, (shape, shape), (far, a, a_come, b, b_come), smem=1)
+    return call(choose_kernel, (pltpu.HBM(a.shape, BF16),) * 2, (far, a, a_come, b, b_come), smem=1)
 
 
 def attend_kernel(position_ref, q_ref, k_ref, v_ref, kp_ref, vp_ref, out_ref):
@@ -372,18 +370,44 @@
     return lax.ppermute(x, axis, [(0, 1), (1, 0)])
 
 
+def half_sum_kernel(own_ref, come_ref, out_ref):
+    for j in range(own_ref.shape[0]):
+        out_ref[j] = (own_ref[j].astype(F32) + come_ref[j].astype(F32)).astype(BF16)
+
+
 def half_sum(own, come):
-    return (own.astype(F32) + come.astype(F32)).astype(BF16)
-
-
-def block_sum(half):
-    arrived = lax.all_to_all(half, CHIPS, 0, 0, tiled=True)
-    return arrived.astype(F32).sum(axis=0).astype(BF16)
-
-
-def from_every_chip(share):
-    copies = jnp.broadcast_to(share, (lax.axis_size(CHIPS), *share.shape))
-    return lax.all_to_all(near(copies), CHIPS, 0, 0, tiled=True)
+    return call(half_sum_kernel, pltpu.VMEM(own.shape, BF16), (own, near(come)))
+
+
+def share_kernel(parts_ref, *out_refs):
+    total = parts_ref[0].astype(F32)
+    for j in range(1, parts_ref.shape[0]):
+        total += parts_ref[j].astype(F32)
+    total = total.astype(BF16)
+    (out_ref,) = out_refs
+    if out_ref.shape == total.shape:
+        out_ref[...] = total
+    else:
+        for j in range(out_ref.shape[0]):
+            out_ref[j] = total
+
+
+def exchanged(blocks):
+    return lax.all_to_all(blocks, CHIPS, 0, 0, tiled=True)
+
+
+def share_of(parts, spread):
+    shape = parts.shape if spread else parts.shape[1:]
+    return call(share_kernel, pltpu.VMEM(shape, BF16), (near(parts),))
+
+
+def copies_kernel(share_ref, out_ref):
+    for j in range(out_ref.shape[0]):
+        out_ref[j] = share_ref[...]
+
+
+def copies_of(share):
+    return call(copies_kernel, pltpu.VMEM((lax.axis_size(CHIPS), *share.shape), BF16), (near(share),))
 
 
 def near(x):
@@ -418,16 +442,16 @@
     weights = tuple(map(stored, (w_gate, w_up, w_down)))
 
     route = [(i, i + 1) for i in range(seats - 1)]
-    k_prior = lax.ppermute(att_k, SEQ, route)
-    v_prior = lax.ppermute(att_v, SEQ, route)
+    k_prior = lax.ppermute(stored(att_k), SEQ, route)
+    v_prior = lax.ppermute(stored(att_v), SEQ, route)
 
     own, away = gradients(core, fast_k, fast_v, rates, weights, chips)
-    share = block_sum(half_sum(own, swap(away, "core")))
+    share = share_of(exchanged(half_sum(own, swap(away, "core"))), False)
     given = lax.ppermute(share, "span", [(0, 1)])
     k_prior, v_prior, share = together(k_prior, v_prior, share)
     attended = attend(position, att_q, att_k, att_v, near(k_prior), near(v_prior))
     given, attended = together(given, attended)
-    own = from_every_chip(given)
+    own = exchanged(copies_of(given))
     weights, own, away = update(core, rates, near(own), near(swap(own, "core")), weights, fast_k, fast_v)
 
     sent = ((0, 1), (0, 2), (1, 3), (1, 2))
@@ -438,12 +462,14 @@
     a_come = flip(a_sent, 1)
     b_come = flip(b_sent, 3)
     a_held, b_held = later_products(held, line, x, rows, w_out, heads)
-    share = block_sum(half_sum(own, come))
-    a_held, a_sent, b_held, b_sent = halve(a_held, near(a_come), b_held, near(b_come))
+    half = half_sum(own, come)
+    parts = exchanged(half)
+    a_held, a_sent, b_held, b_sent = halve(a_held, a_come, b_held, b_come)
     a_come = flip(a_sent, 3)
     b_come = flip(b_sent, 1)
-    own = from_every_chip(share)
-    held, sent = choose(far, a_held, near(a_come), b_held, near(b_come))
+    copies = share_of(parts, True)
+    own = exchanged(copies)
+    held, sent = choose(far, a_held, a_come, b_held, b_come)
     come = swap(sent, HEAD[0])
     away = swap(own, "core")
 

time: 156 us -> 154 us (0.987)
  Pallas kernels: 35.5 us -> 39.4 us
  other arithmetic: 5.68 us -> 2.43 us
  local copies, waits for them, and re-layouts: 6.17 us -> 3.64 us
    pallas_call x3 -> x8, Pallas kernels: 6.27 us -> 10.1 us  [call(): pl.pallas_call(kernel, out_shape=outs, in_specs=[SMEM] * smem + [VMEM] *...]
    convert_element_type x2 -> x0, other arithmetic: 3.03 us -> none  [half_sum(): return (own.astype(F32) + come.astype(F32)).astype(BF16)]
    unnamed x22 -> x14, local copies, waits for them, and re-layouts: 5.11 us -> 3.64 us
  transfers between devices with their start and end apart: 15 -> 15, of which waited for: 8 -> 9; matrix products, arithmetic and copies ran while one was open for 1% -> 1% of each run, Pallas kernels for 14% -> 14%
where the time goes in v2:
time: 154 us; the launch traced here: 153 us
  Pallas kernels  39.4 us (26%)
  blocking collectives  37.7 us (24%)
  waiting for transfers between devices  34.8 us (23%)
  starting transfers between devices  33.8 us (22%)
  local copies, waits for them, and re-layouts  3.64 us (2%)
  other arithmetic  2.43 us (2%)
    all_to_all x2, blocking collectives, exchanged(): return lax.all_to_all(blocks, CHIPS, 0, 0, tiled=True)  37.7 us
    ppermute x4, waiting for transfers between devices, flip(): return lax.ppermute(x, HEAD[1], [(i, i ^ mask) for i in devices])  12.7 us
    all_to_all x2, waiting for transfers between devices, exchanged(): return lax.all_to_all(blocks, CHIPS, 0, 0, tiled=True)  12.7 us
    all_to_all x2, starting transfers between devices, exchanged(): return lax.all_to_all(blocks, CHIPS, 0, 0, tiled=True)  11.4 us
    pallas_call x1, Pallas kernels, update(): pl.pallas_call(update_kernel, compiler_params=ROOM, out_shape=(weight,) *...  10.6 us
    pallas_call x8, Pallas kernels, call(): pl.pallas_call(kernel, out_shape=outs, in_specs=[SMEM] * smem + [VMEM] *...  10.1 us
    pallas_call x1, Pallas kernels, last_update(): pl.pallas_call(last_kernel, out_shape=(shape, shape), in_specs=[SMEM, SME...  8.08 us
    ppermute x4, starting transfers between devices, flip(): return lax.ppermute(x, HEAD[1], [(i, i ^ mask) for i in devices])  5.69 us
  transfers between devices with their start and end apart: 15, of which 9 were waited for; matrix products, arithmetic and copies ran while one was open for 1% of the time, Pallas kernels for 14%

profile of v2, /device:TPU:8, one launch (start us, length us, event | category | flops | bytes accessed | tf_op | source)
XLA Modules:
  0.0 152.5 jit_solution(11538245797084754406)
XLA Ops:
  0.6 0.0 copy-start.1
  0.6 0.0 copy-start.2
  0.7 0.0 copy-start
  0.7 4.1 %shard_map.122 = (bf16[8,3,32,512]{3,2,1,0:T(8,128)(2,1)S(1)}, bf16[8,3,32,512]{3,2,1,0:T(8,128)(2,1)S(1)}) custom-call(s32[1]{0:T(128)} %bitcast.core_ref, f32[1,256]{1,0:T(1,128)} %rate_in.3, bf16[256,512]{1,0:T(8,128)(2,1)} %k_in.3, bf16[256,512]{1,0:T(8,128)(2,1)} %v_in.3, bf16[1,512,512]{2,1,0:T(8,128)(2,1)} %wg_in.3, bf16[1,512,512]{2,1,0:T(8,128)(2,1)} %wu_in.3, ...), custom_call_target="tpu_custom_call" | custom-call | tf_op jit(solution)/shard_map/pallas_call | solution.py:122
  4.8 0.1 collective-permute-start
  4.9 2.3 %collective-permute-done.come_ref = bf16[8,3,32,512]{3,2,1,0:T(8,128)(2,1)S(1)} collective-permute-done((bf16[8,3,32,512]{3,2,1,0:T(8,128)(2,1)S(1)}, bf16[8,3,32,512]{3,2,1,0:T(8,128)(2,1)S(1)}, u32[]{:S(2)}, u32[]{:S(2)}) %collective-permute-start) | collective-permute-done | bytes 786464 | tf_op jit(solution)/shard_map/ppermute | solution.py:370
  7.2 1.1 shard_map.123
  8.2 6.3 %all-to-all-start = ((bf16[8,3,32,512]{3,2,1,0:T(8,128)(2,1)}), bf16[8,3,32,512]{3,2,1,0:T(8,128)(2,1)S(1)}, u32[]{:S(2)}, u32[]{:S(2)}) async-start(bf16[8,3,32,512]{3,2,1,0:T(8,128)(2,1)} %shard_map.123), calls=%async_computation | async-start | bytes 1572864 | tf_op jit(solution)/shard_map/all_to_all | solution.py:396
  14.5 0.0 copy-done.1
  14.5 1.9 %collective-permute-start.2 = (bf16[256,640]{1,0:T(8,128)(2,1)S(1)}, bf16[256,640]{1,0:T(8,128)(2,1)S(1)}, u32[]{:S(2)}, u32[]{:S(2)}) collective-permute-start(bf16[256,640]{1,0:T(8,128)(2,1)S(1)} %copy-done.1), channel_id=1, source_target_pairs={{0,8},{8,16},{16,24},{24,32},{32,40},{40,48},{48,56},{56,64},{64,7... | collective-permute-start | bytes 983048 | tf_op jit(solution)/shard_map/ppermute | solution.py:445
  16.4 0.0 copy-done.2
  16.4 3.5 %collective-permute-start.3 = (bf16[256,640]{1,0:T(8,128)(2,1)S(1)}, bf16[256,640]{1,0:T(8,128)(2,1)S(1)}, u32[]{:S(2)}, u32[]{:S(2)}) collective-permute-start(bf16[256,640]{1,0:T(8,128)(2,1)S(1)} %copy-done.2), channel_id=1, source_target_pairs={{0,8},{8,16},{16,24},{24,32},{32,40},{40,48},{48,56},{56,64},{64,7... | collective-permute-start | bytes 983048 | tf_op jit(solution)/shard_map/ppermute | solution.py:446
  19.9 5.7 %all-to-all-done.parts_ref = bf16[8,3,32,512]{3,2,1,0:T(8,128)(2,1)S(1)} async-done(((bf16[8,3,32,512]{3,2,1,0:T(8,128)(2,1)}), bf16[8,3,32,512]{3,2,1,0:T(8,128)(2,1)S(1)}, u32[]{:S(2)}, u32[]{:S(2)}) %all-to-all-start) | async-done | bytes 786464 | tf_op jit(solution)/shard_map/all_to_all | solution.py:396
  25.6 0.1 shard_map.124
  25.7 5.2 %collective-permute-start.1 = (bf16[3,32,512]{2,1,0:T(8,128)(2,1)S(1)}, bf16[3,32,512]{2,1,0:T(8,128)(2,1)S(1)}, u32[]{:S(2)}, u32[]{:S(2)}) collective-permute-start(bf16[3,32,512]{2,1,0:T(8,128)(2,1)S(1)} %shard_map.124), channel_id=1, source_target_pairs={{0,128},{1,129},{2,130},{3,131},{4,132},{5,133},{6,134},{7,135},{8... | collective-permute-start | bytes 294920 | tf_op jit(solution)/shard_map/ppermute | solution.py:450
  30.9 0.0 collective-permute-done.2.kp_ref
  31.0 0.0 collective-permute-done.3.vp_ref
  31.0 0.0 copy-done
  31.0 2.2 %shard_map.125 = f32[256,640]{1,0:T(8,128)S(1)} custom-call(s32[1]{0:T(128)} %bitcast.1.position_ref, bf16[256,640]{1,0:T(8,128)(2,1)S(1)} %copy-done, bf16[256,640]{1,0:T(8,128)(2,1)S(1)} %copy-done.1, bf16[256,640]{1,0:T(8,128)(2,1)S(1)} %copy-done.2, bf16[256,640]{1,0:T(8,128)(2,1)S(1)} %collective-permute-done.2.kp_ref, ...), custom_call_target="tpu_custom_call" | custom-call | tf_op jit(solution)/shard_map/pallas_call | solution.py:40
  33.2 0.0 collective-permute-done.1.share_ref
  33.2 0.1 shard_map.126
  33.2 21.6 %all_to_all.20.own_in = bf16[8,3,32,512]{3,2,1,0:T(8,128)(2,1)S(1)} all-to-all(bf16[8,3,32,512]{3,2,1,0:T(8,128)(2,1)S(1)} %shard_map.126), channel_id=1, replica_groups=mesh['span'=2,'row'=2,'y'=4,'core'=2,'head_0'=2,'head_1'=4] {'row','y'}, dimensions={0} | all-to-all | bytes 1572864 | tf_op jit(solution)/shard_map/all_to_all | solution.py:396
  54.9 0.0 collective-permute-start.4
  54.9 2.3 %collective-permute-done.4.far_in = bf16[8,3,32,512]{3,2,1,0:T(8,128)(2,1)S(1)} collective-permute-done((bf16[8,3,32,512]{3,2,1,0:T(8,128)(2,1)S(1)}, bf16[8,3,32,512]{3,2,1,0:T(8,128)(2,1)S(1)}, u32[]{:S(2)}, u32[]{:S(2)}) %collective-permute-start.4) | collective-permute-done | bytes 786464 | tf_op jit(solution)/shard_map/ppermute | solution.py:370
  57.1 10.6 %shard_map.127 = (bf16[1,512,512]{2,1,0:T(8,128)(2,1)S(1)}, bf16[1,512,512]{2,1,0:T(8,128)(2,1)S(1)}, bf16[1,512,512]{2,1,0:T(8,128)(2,1)S(1)}, bf16[8,3,32,512]...) custom-call(s32[1]{0:T(128)} %bitcast.core_ref, f32[1,256]{1,0:T(1,128)} %rate_in.3, ...), custom_call_target="tpu_custom_call" | custom-call | tf_op jit(solution)/shard_map/pallas_call | solution.py:202
  67.8 0.2 collective-permute-start.5
  68.0 3.8 %shard_map.128 = (bf16[2,256,640]{2,1,0:T(8,128)(2,1)S(1)}, bf16[2,256,640]{2,1,0:T(8,128)(2,1)S(1)}, bf16[256,512]{1,0:T(8,128)(2,1)S(1)}) custom-call(s32[1]{0:T(128)} %bitcast.3.x_ref, bf16[256,512]{1,0:T(8,128)(2,1)} %q_in.1, bf16[1,512,512]{2,1,0:T(8,128)(2,1)S(1)} %get-tuple-element.37.wg_ref, bf16[1,512,512]{2,1,0:T(8,128)(2,1)S(1)} %get-tuple-element.38.wu_ref, ...), custom_call_target="tpu_custom_call" | custom-call | tf_op jit(solution)/shard_map/pallas_call | solution.py:292
  71.8 0.0 copy-start.5
  71.9 0.9 copy-done.5
  72.7 0.0 copy-start.6
  72.7 0.8 copy-done.6
  73.5 0.0 collective-permute-done.5.come_ref
  73.5 1.3 shard_map.132
  74.9 16.0 %all_to_all.21.parts_ref = bf16[8,3,32,512]{3,2,1,0:T(8,128)(2,1)S(1)} all-to-all(bf16[8,3,32,512]{3,2,1,0:T(8,128)(2,1)S(1)} %shard_map.132), channel_id=1, replica_groups=mesh['span'=2,'row'=2,'y'=4,'core'=2,'head_0'=2,'head_1'=4] {'row','y'}, dimensions={0} | all-to-all | bytes 1572864 | tf_op jit(solution)/shard_map/all_to_all | solution.py:396
  90.9 1.0 shard_map.133
  91.9 5.1 %all-to-all-start.3 = ((bf16[8,3,32,512]{3,2,1,0:T(8,128)(2,1)}), bf16[8,3,32,512]{3,2,1,0:T(8,128)(2,1)S(1)}, u32[]{:S(2)}, u32[]{:S(2)}) async-start(bf16[8,3,32,512]{3,2,1,0:T(8,128)(2,1)} %shard_map.133), calls=%async_computation.3 | async-start | bytes 1572864 | tf_op jit(solution)/shard_map/all_to_all | solution.py:396
  97.0 1.5 collective-permute-start.6
  98.5 2.1 %collective-permute-start.7 = (bf16[2,256,640]{2,1,0:T(8,128)(2,1)}, bf16[2,256,640]{2,1,0:T(8,128)(2,1)}, u32[]{:S(2)}, u32[]{:S(2)}) collective-permute-start(bf16[2,256,640]{2,1,0:T(8,128)(2,1)} %copy-done.5), channel_id=1, source_target_pairs={{0,3},{1,2},{2,1},{3,0},{4,7},{5,6},{6,5},{7,4},{8,11},{9,10},{10,... | collective-permute-start | bytes 1966088 | tf_op jit(solution)/shard_map/ppermute | solution.py:427
  100.6 7.0 %all-to-all-done.3.own_in = bf16[8,3,32,512]{3,2,1,0:T(8,128)(2,1)S(1)} async-done(((bf16[8,3,32,512]{3,2,1,0:T(8,128)(2,1)}), bf16[8,3,32,512]{3,2,1,0:T(8,128)(2,1)S(1)}, u32[]{:S(2)}, u32[]{:S(2)}) %all-to-all-start.3) | async-done | bytes 786464 | tf_op jit(solution)/shard_map/all_to_all | solution.py:396
  107.6 0.0 collective-permute-start.11
  107.6 2.6 %shard_map.129 = (bf16[2,256,640]{2,1,0:T(8,128)(2,1)S(1)}, bf16[2,256,640]{2,1,0:T(8,128)(2,1)S(1)}) custom-call(s32[1]{0:T(128)} %bitcast.3.x_ref, bf16[256,512]{1,0:T(8,128)(2,1)S(1)} %get-tuple-element.43.rows_ref, bf16[512,5120]{1,0:T(8,128)(2,1)} %wo_in.3), custom_call_target="tpu_custom_call" | custom-call | tf_op jit(solution)/shard_map/pallas_call | solution.py:311
  110.2 2.8 %collective-permute-done.6.ar_ref = bf16[2,256,640]{2,1,0:T(8,128)(2,1)} collective-permute-done((bf16[2,256,640]{2,1,0:T(8,128)(2,1)}, bf16[2,256,640]{2,1,0:T(8,128)(2,1)}, u32[]{:S(2)}, u32[]{:S(2)}) %collective-permute-start.6) | collective-permute-done | bytes 655392 | tf_op jit(solution)/shard_map/ppermute | solution.py:427
  113.0 2.4 %collective-permute-done.7.br_ref = bf16[2,256,640]{2,1,0:T(8,128)(2,1)} collective-permute-done((bf16[2,256,640]{2,1,0:T(8,128)(2,1)}, bf16[2,256,640]{2,1,0:T(8,128)(2,1)}, u32[]{:S(2)}, u32[]{:S(2)}) %collective-permute-start.7) | collective-permute-done | bytes 655392 | tf_op jit(solution)/shard_map/ppermute | solution.py:427
  115.4 2.4 %shard_map.130 = (bf16[256,640]{1,0:T(8,128)(2,1)}, bf16[256,640]{1,0:T(8,128)(2,1)}, bf16[256,640]{1,0:T(8,128)(2,1)}, bf16[256,640]{1,0:T(8,128)(2,1)}) custom-call(bf16[2,256,640]{2,1,0:T(8,128)(2,1)S(1)} %get-tuple-element.44.a_ref, bf16[2,256,640]{2,1,0:T(8,128)(2,1)} %collective-permute-done.6.ar_ref, ...), custom_call_target="tpu_custom_call" | custom-call | tf_op jit(solution)/shard_map/pallas_call | solution.py:40
  117.8 2.1 %collective-permute-start.8 = (bf16[256,640]{1,0:T(8,128)(2,1)}, bf16[256,640]{1,0:T(8,128)(2,1)S(1)}, u32[]{:S(2)}, u32[]{:S(2)}) collective-permute-start(bf16[256,640]{1,0:T(8,128)(2,1)} %get-tuple-element.49), channel_id=1, source_target_pairs={{0,3},{1,2},{2,1},{3,0},{4,7},{5,6},{6,5},{7,4},{8,11},{9,10},{10,... | collective-permute-start | bytes 983048 | tf_op jit(solution)/shard_map/ppermute | solution.py:427
  119.9 0.0 collective-permute-start.9
  119.9 6.8 %collective-permute-done.8.ar_ref = bf16[256,640]{1,0:T(8,128)(2,1)S(1)} collective-permute-done((bf16[256,640]{1,0:T(8,128)(2,1)}, bf16[256,640]{1,0:T(8,128)(2,1)S(1)}, u32[]{:S(2)}, u32[]{:S(2)}) %collective-permute-start.8) | collective-permute-done | bytes 327712 | tf_op jit(solution)/shard_map/ppermute | solution.py:427
  126.7 0.7 collective-permute-done.9.br_ref
  127.4 0.0 copy-start.3
  127.4 1.0 copy-done.3
  128.4 0.0 copy-start.4
  128.4 1.0 copy-done.4
  129.4 2.0 %shard_map.131 = (bf16[256,640]{1,0:T(8,128)(2,1)}, bf16[256,640]{1,0:T(8,128)(2,1)}) custom-call(s32[1]{0:T(128)} %bitcast.2.far_ref, bf16[256,640]{1,0:T(8,128)(2,1)S(1)} %copy-done.3, bf16[256,640]{1,0:T(8,128)(2,1)S(1)} %collective-permute-done.8.ar_ref, bf16[256,640]{1,0:T(8,128)(2,1)S(1)} %copy-done.4, bf16[256,640]{1,0:T(8,128)(2,1)} %collective-permute-done.9.br_ref), custom_call_target="tpu_custom_call" | custom-call | tf_op jit(solution)/shard_map/pallas_call | solution.py:40
  131.4 4.5 %collective-permute-start.10 = (bf16[256,640]{1,0:T(8,128)(2,1)}, bf16[256,640]{1,0:T(8,128)(2,1)S(1)}, u32[]{:S(2)}, u32[]{:S(2)}) collective-permute-start(bf16[256,640]{1,0:T(8,128)(2,1)} %get-tuple-element.53), channel_id=1, source_target_pairs={{0,4},{4,0},{1,5},{5,1},{2,6},{6,2},{3,7},{7,3},{8,12},{12,8},{9,1... | collective-permute-start | bytes 983048 | tf_op jit(solution)/shard_map/ppermute | solution.py:370
  135.9 0.0 collective-permute-done.11.far_in
  135.9 8.1 %shard_map.134 = (bf16[3,16,512]{2,1,0:T(8,128)(2,1)S(1)}, bf16[3,16,512]{2,1,0:T(8,128)(2,1)S(1)}) custom-call(s32[1]{0:T(128)} %bitcast.core_ref, s32[1]{0:T(128)} %bitcast.4.seat_ref, bf16[8,3,32,512]{3,2,1,0:T(8,128)(2,1)S(1)} %all-to-all-done.3.own_in, bf16[8,3,32,512]{3,2,1,0:T(8,128)(2,1)} %collective-permute-done.11.far_in, ...), custom_call_target="tpu_custom_call" | custom-call | tf_op jit(solution)/shard_map/pallas_call | solution.py:237
  144.0 1.3 collective-permute-start.12
  145.3 0.0 collective-permute-done.10
  145.3 1.8 %add_convert_fusion = bf16[256,640]{1,0:T(8,128)(2,1)} fusion(bf16[256,640]{1,0:T(8,128)(2,1)S(1)} %collective-permute-done.10, f32[256,640]{1,0:T(8,128)S(1)} %shard_map.125, bf16[256,640]{1,0:T(8,128)(2,1)} %get-tuple-element.52), kind=kLoop, calls=%fused_computation | loop fusion | flops 819200 | bytes 1638400 | tf_op jit(solution)/shard_map/convert_element_type | solution.py:479
  147.1 4.8 %collective-permute-done.12 = bf16[3,16,512]{2,1,0:T(8,128)(2,1)S(1)} collective-permute-done((bf16[3,16,512]{2,1,0:T(8,128)(2,1)S(1)}, bf16[3,16,512]{2,1,0:T(8,128)(2,1)S(1)}, u32[]{:S(2)}, u32[]{:S(2)}) %collective-permute-start.12) | collective-permute-done | bytes 49184 | tf_op jit(solution)/shard_map/ppermute | solution.py:477
  151.9 0.6 select_bitcast_fusion
Async XLA Ops:
  0.6 13.9 %copy-start.1 = (bf16[256,640]{1,0:T(8,128)(2,1)S(1)}, bf16[256,640]{1,0:T(8,128)(2,1)}, u32[]{:S(2)}) copy-start(bf16[256,640]{1,0:T(8,128)(2,1)} %k_ref.1) | copy-start | bytes 983044
  0.6 15.8 %copy-start.2 = (bf16[256,640]{1,0:T(8,128)(2,1)S(1)}, bf16[256,640]{1,0:T(8,128)(2,1)}, u32[]{:S(2)}) copy-start(bf16[256,640]{1,0:T(8,128)(2,1)} %v_ref.1) | copy-start | bytes 983044
  0.7 30.3 %copy-start = (bf16[256,640]{1,0:T(8,128)(2,1)S(1)}, bf16[256,640]{1,0:T(8,128)(2,1)}, u32[]{:S(2)}) copy-start(bf16[256,640]{1,0:T(8,128)(2,1)} %q_ref.1) | copy-start | bytes 983044
  4.8 2.4 %collective-permute-start = (bf16[8,3,32,512]{3,2,1,0:T(8,128)(2,1)S(1)}, bf16[8,3,32,512]{3,2,1,0:T(8,128)(2,1)S(1)}, u32[]{:S(2)}, u32[]{:S(2)}) collective-permute-start(bf16[8,3,32,512]{3,2,1,0:T(8,128)(2,1)S(1)} %get-tuple-element.31), channel_id=1, source_target_pairs={{0,8},{8,0},{1,9},{9,1},{2,10},{10,2},{3,11},{11,3},{4,12},{12,4},... | collective-permute-start | bytes 2359304 | tf_op jit(solution)/shard_map/ppermute | solution.py:370
  8.2 17.4 %all-to-all-start = ((bf16[8,3,32,512]{3,2,1,0:T(8,128)(2,1)}), bf16[8,3,32,512]{3,2,1,0:T(8,128)(2,1)S(1)}, u32[]{:S(2)}, u32[]{:S(2)}) async-start(bf16[8,3,32,512]{3,2,1,0:T(8,128)(2,1)} %shard_map.123), calls=%async_computation | async-start | bytes 1572864 | tf_op jit(solution)/shard_map/all_to_all | solution.py:396
  14.5 16.4 %collective-permute-start.2 = (bf16[256,640]{1,0:T(8,128)(2,1)S(1)}, bf16[256,640]{1,0:T(8,128)(2,1)S(1)}, u32[]{:S(2)}, u32[]{:S(2)}) collective-permute-start(bf16[256,640]{1,0:T(8,128)(2,1)S(1)} %copy-done.1), channel_id=1, source_target_pairs={{0,8},{8,16},{16,24},{24,32},{32,40},{40,48},{48,56},{56,64},{64,7... | collective-permute-start | bytes 983048 | tf_op jit(solution)/shard_map/ppermute | solution.py:445
  16.4 14.5 %collective-permute-start.3 = (bf16[256,640]{1,0:T(8,128)(2,1)S(1)}, bf16[256,640]{1,0:T(8,128)(2,1)S(1)}, u32[]{:S(2)}, u32[]{:S(2)}) collective-permute-start(bf16[256,640]{1,0:T(8,128)(2,1)S(1)} %copy-done.2), channel_id=1, source_target_pairs={{0,8},{8,16},{16,24},{24,32},{32,40},{40,48},{48,56},{56,64},{64,7... | collective-permute-start | bytes 983048 | tf_op jit(solution)/shard_map/ppermute | solution.py:446
  25.7 7.4 %collective-permute-start.1 = (bf16[3,32,512]{2,1,0:T(8,128)(2,1)S(1)}, bf16[3,32,512]{2,1,0:T(8,128)(2,1)S(1)}, u32[]{:S(2)}, u32[]{:S(2)}) collective-permute-start(bf16[3,32,512]{2,1,0:T(8,128)(2,1)S(1)} %shard_map.124), channel_id=1, source_target_pairs={{0,128},{1,129},{2,130},{3,131},{4,132},{5,133},{6,134},{7,135},{8... | collective-permute-start | bytes 294920 | tf_op jit(solution)/shard_map/ppermute | solution.py:450
  54.9 2.3 %collective-permute-start.4 = (bf16[8,3,32,512]{3,2,1,0:T(8,128)(2,1)S(1)}, bf16[8,3,32,512]{3,2,1,0:T(8,128)(2,1)S(1)}, u32[]{:S(2)}, u32[]{:S(2)}) collective-permute-start(bf16[8,3,32,512]{3,2,1,0:T(8,128)(2,1)S(1)} %all_to_all.20.own_in), channel_id=1, source_target_pairs={{0,8},{8,0},{1,9},{9,1},{2,10},{10,2},{3,11},{11,3},{4,12},{12,4},... | collective-permute-start | bytes 2359304 | tf_op jit(solution)/shard_map/ppermute | solution.py:370
  67.8 5.8 %collective-permute-start.5 = (bf16[8,3,32,512]{3,2,1,0:T(8,128)(2,1)}, bf16[8,3,32,512]{3,2,1,0:T(8,128)(2,1)}, u32[]{:S(2)}, u32[]{:S(2)}) collective-permute-start(bf16[8,3,32,512]{3,2,1,0:T(8,128)(2,1)} %get-tuple-element.36), channel_id=1, source_target_pairs={{0,8},{8,0},{1,9},{9,1},{2,10},{10,2},{3,11},{11,3},{4,12},{12,4},... | collective-permute-start | bytes 2359304 | tf_op jit(solution)/shard_map/ppermute | solution.py:370
  71.8 0.9 copy-start.5
  72.7 0.8 copy-start.6
  91.9 15.7 %all-to-all-start.3 = ((bf16[8,3,32,512]{3,2,1,0:T(8,128)(2,1)}), bf16[8,3,32,512]{3,2,1,0:T(8,128)(2,1)S(1)}, u32[]{:S(2)}, u32[]{:S(2)}) async-start(bf16[8,3,32,512]{3,2,1,0:T(8,128)(2,1)} %shard_map.133), calls=%async_computation.3 | async-start | bytes 1572864 | tf_op jit(solution)/shard_map/all_to_all | solution.py:396
  97.0 16.0 %collective-permute-start.6 = (bf16[2,256,640]{2,1,0:T(8,128)(2,1)}, bf16[2,256,640]{2,1,0:T(8,128)(2,1)}, u32[]{:S(2)}, u32[]{:S(2)}) collective-permute-start(bf16[2,256,640]{2,1,0:T(8,128)(2,1)} %copy-done.6), channel_id=1, source_target_pairs={{0,1},{1,0},{2,3},{3,2},{4,5},{5,4},{6,7},{7,6},{8,9},{9,8},{10,11... | collective-permute-start | bytes 1966088 | tf_op jit(solution)/shard_map/ppermute | solution.py:427
  98.5 16.9 %collective-permute-start.7 = (bf16[2,256,640]{2,1,0:T(8,128)(2,1)}, bf16[2,256,640]{2,1,0:T(8,128)(2,1)}, u32[]{:S(2)}, u32[]{:S(2)}) collective-permute-start(bf16[2,256,640]{2,1,0:T(8,128)(2,1)} %copy-done.5), channel_id=1, source_target_pairs={{0,3},{1,2},{2,1},{3,0},{4,7},{5,6},{6,5},{7,4},{8,11},{9,10},{10,... | collective-permute-start | bytes 1966088 | tf_op jit(solution)/shard_map/ppermute | solution.py:427
  107.6 28.3 %collective-permute-start.11 = (bf16[8,3,32,512]{3,2,1,0:T(8,128)(2,1)S(1)}, bf16[8,3,32,512]{3,2,1,0:T(8,128)(2,1)}, u32[]{:S(2)}, u32[]{:S(2)}) collective-permute-start(bf16[8,3,32,512]{3,2,1,0:T(8,128)(2,1)S(1)} %all-to-all-done.3.own_in), channel_id=1, source_target_pairs={{0,8},{8,0},{1,9},{9,1},{2,10},{10,2},{3,11},{11,3},{4,12},{12,4},... | collective-permute-start | bytes 2359304 | tf_op jit(solution)/shard_map/ppermute | solution.py:370
  117.8 8.9 %collective-permute-start.8 = (bf16[256,640]{1,0:T(8,128)(2,1)}, bf16[256,640]{1,0:T(8,128)(2,1)S(1)}, u32[]{:S(2)}, u32[]{:S(2)}) collective-permute-start(bf16[256,640]{1,0:T(8,128)(2,1)} %get-tuple-element.49), channel_id=1, source_target_pairs={{0,3},{1,2},{2,1},{3,0},{4,7},{5,6},{6,5},{7,4},{8,11},{9,10},{10,... | collective-permute-start | bytes 983048 | tf_op jit(solution)/shard_map/ppermute | solution.py:427
  119.9 7.5 %collective-permute-start.9 = (bf16[256,640]{1,0:T(8,128)(2,1)}, bf16[256,640]{1,0:T(8,128)(2,1)}, u32[]{:S(2)}, u32[]{:S(2)}) collective-permute-start(bf16[256,640]{1,0:T(8,128)(2,1)} %get-tuple-element.51), channel_id=1, source_target_pairs={{0,1},{1,0},{2,3},{3,2},{4,5},{5,4},{6,7},{7,6},{8,9},{9,8},{10,11... | collective-permute-start | bytes 983048 | tf_op jit(solution)/shard_map/ppermute | solution.py:427
  127.4 1.0 copy-start.3
  128.4 1.0 copy-start.4
  131.4 13.9 %collective-permute-start.10 = (bf16[256,640]{1,0:T(8,128)(2,1)}, bf16[256,640]{1,0:T(8,128)(2,1)S(1)}, u32[]{:S(2)}, u32[]{:S(2)}) collective-permute-start(bf16[256,640]{1,0:T(8,128)(2,1)} %get-tuple-element.53), channel_id=1, source_target_pairs={{0,4},{4,0},{1,5},{5,1},{2,6},{6,2},{3,7},{7,3},{8,12},{12,8},{9,1... | collective-permute-start | bytes 983048 | tf_op jit(solution)/shard_map/ppermute | solution.py:370
  144.0 8.0 %collective-permute-start.12 = (bf16[3,16,512]{2,1,0:T(8,128)(2,1)S(1)}, bf16[3,16,512]{2,1,0:T(8,128)(2,1)S(1)}, u32[]{:S(2)}, u32[]{:S(2)}) collective-permute-start(bf16[3,16,512]{2,1,0:T(8,128)(2,1)S(1)} %get-tuple-element.57), channel_id=1, source_target_pairs={{128,0},{129,1},{130,2},{131,3},{132,4},{133,5},{134,6},{135,7},{1... | collective-permute-start | bytes 147464 | tf_op jit(solution)/shard_map/ppermute | solution.py:477
